TPU v7x, 512 devices: a whole 4x4x16 slice. The times are simulated.
512 devices in a mesh: root: 4 (over z_hi, core), col: 128 (over z_lo, y, x).
Axes of the slice: x: 4, y: 4, z: 16 (z_hi: 2, z_lo: 8; z = z_hi * 8 + z_lo), core: 2. Of those that a mesh axis runs over, the one named last changes fastest.
Arguments:
- coeffs: float32 [4, 3072, 3072], P('root', 'col'), may hold values from -6 to 6
- diagonal: float32 [3072, 3072], P('col'), may hold values from -1 to 1
- shift: float32 [4], P('root'), may hold values from -1 to 1
- rotation: float32 [4, 4], replicated, may hold values from -1 to 1, as said below
- string_blocks: bfloat16 [30720, 128], P('col'), may hold values from -0.15625 to 0.15625
- block_cols: int32 [24, 10], replicated, may hold values from 0 to 23, all different within a row
Outputs:
- filtered: float32 [4, 3072, 3072], P('root', 'col')
Inputs may be any that keep to these rules, and one draw needn't show every extreme that they name: `block_cols`: each row names 10 different block columns, and every block column is named by some row. rotation is an orthogonal matrix.
All inputs are finite; a program needn't handle non-finite values.
Results may differ from a plain program's by a relative error of at most 0.0003.
Values may be sent and summed in bfloat16 or wider, within the bound.
A program may use at most 64 MiB of HBM per device.

v0:
```python
import jax
import jax.numpy as jnp
from jax import lax
from jax.sharding import PartitionSpec as P


def apply_blocks(matrix, operator_blocks, block_cols):
    height, breadth = matrix.shape
    nblocks, filled = block_cols.shape
    blocksize = breadth // nblocks
    grouped = matrix.reshape(height, nblocks, blocksize)
    picked = jnp.take(grouped, block_cols, axis=1)
    tiles = operator_blocks.reshape(nblocks, filled, blocksize, blocksize).astype(jnp.float32)
    result = jnp.einsum("rifk,ifjk->rij", picked, tiles, precision=lax.Precision.HIGHEST)
    return result.reshape(height, breadth)


def layout_pieces(stacked):
    count, height, breadth = stacked.shape
    groups = breadth // height
    return (
        stacked.reshape(count, height, groups, height)
        .transpose(0, 2, 1, 3)
        .reshape(count, groups, height * height)
    )


def layout_whole(moved, height):
    count = moved.shape[0]
    groups = moved.shape[1]
    return (
        moved.reshape(count, groups, height, height)
        .transpose(0, 3, 1, 2)
        .reshape(count, height, groups * height)
    )


def swap_layout(stacked):
    moved = lax.all_to_all(layout_pieces(stacked), "col", split_axis=1, concat_axis=1, tiled=True)
    return layout_whole(moved, stacked.shape[1])


def shards(coeffs, diagonal, shift, rotation, string_blocks, block_cols):
    start = coeffs[0]
    energy = shift[0]
    operator_blocks = lax.all_gather(string_blocks, "col", axis=0, tiled=True)

    def apply_local(matrix):
        return apply_blocks(matrix, operator_blocks, block_cols)

    def sigma_local(vector):
        turned = swap_layout(vector[None])[0]
        beta_turned = apply_local(turned)
        beta_part = swap_layout(beta_turned[None])[0]
        return apply_local(vector) + beta_part + diagonal * vector

    first = 0.5 * (sigma_local(start) - energy * start)
    second = sigma_local(first) - energy * first - start
    all_roots = lax.all_gather(second[None], "root", axis=0, tiled=True)
    weights = lax.dynamic_index_in_dim(rotation, lax.axis_index("root"), 0, keepdims=False)
    result = jnp.einsum("s,sba->ba", weights, all_roots, precision=lax.Precision.HIGHEST)
    return result[None]


def solution(mesh):
    return jax.shard_map(
        shards,
        mesh=mesh,
        in_specs=(P("root", "col", None), P("col", None), P("root"), P(), P("col", None), P()),
        out_specs=P("root", "col", None),
        check_vma=False,
    )
```

profile of v0, /device:TPU:1, one launch (start us, length us, event | category | flops | bytes accessed | tf_op | source)
XLA Modules:
  0.0 1165.1 jit_solution(13638159206079844193)
XLA Ops:
  7.3 2.1 reshape_broadcast_in_dim_squeeze.3
  9.8 1.0 copy.62
  10.8 20.4 %all-to-all-start = ((f32[1,128,576]{2,0,1:T(1,128)}), f32[1,128,576]{2,0,1:T(1,128)S(1)}, u32[]{:S(2)}, u32[]{:S(2)}) async-start(f32[1,128,576]{2,0,1:T(1,128)} %copy.62), calls=%async_computation | async-start | bytes 655360 | tf_op jit(solution)/shard_map/all_to_all | solution.py:39
  31.5 21.5 %all-to-all-done = f32[1,128,576]{2,0,1:T(1,128)S(1)} async-done(((f32[1,128,576]{2,0,1:T(1,128)}), f32[1,128,576]{2,0,1:T(1,128)S(1)}, u32[]{:S(2)}, u32[]{:S(2)}) %all-to-all-start) | async-done | bytes 294944 | tf_op jit(solution)/shard_map/all_to_all | solution.py:39
  53.6 0.9 reshape_squeeze_reshape.6
  54.6 1.0 gather_fusion.1
  55.6 841.9 %all-gather.4.cloned.1.call-done = bf16[30720,128]{1,0:T(8,128)(2,1)} async-done(((bf16[240,128]{1,0:T(8,128)(2,1)}), bf16[30720,128]{1,0:T(8,128)(2,1)}) %all-gather.4.cloned.1.call-update) | async-done | bytes 7864336 | tf_op jit(solution)/shard_map/all_gather | solution.py:46
  897.5 8.5 fusion.25
  906.2 1.0 reshape_broadcast_in_dim_reshape.6
  907.6 0.9 copy.69
  908.5 7.4 all-to-all-start.1
  916.1 1.0 gather_fusion
  917.8 9.2 fusion.22
  927.0 4.3 all-to-all-done.1
  931.3 1.1 copy.70
  932.9 0.9 squeeze_reshape.6
  935.3 1.1 reshape_broadcast_in_dim.3
  937.1 27.6 %all_to_all.20 = f32[1,128,576]{2,0,1:T(1,128)S(1)} all-to-all(f32[1,128,576]{2,0,1:T(1,128)S(1)} %copy.77), channel_id=1, replica_groups=mesh['root'=4,'col'=128] {'col'}, dimensions={1} | all-to-all | bytes 589824 | tf_op jit(solution)/shard_map/all_to_all | solution.py:39
  965.3 0.9 reshape_squeeze_reshape.7
  966.4 1.0 gather_fusion.3
  967.4 8.6 fusion.31
  976.0 1.0 reshape_broadcast_in_dim_reshape.7
  977.4 0.9 copy.84
  978.4 8.1 all-to-all-start.3
  986.9 1.0 gather_fusion.2
  987.9 9.2 fusion.28
  997.1 4.9 all-to-all-done.3
  1002.0 1.1 copy.85
  1003.6 0.9 squeeze_reshape.7
  1004.5 0.8 fusion.36
  1005.4 148.2 %all-gather.6.cloned.1.call-done = f32[96,3072]{1,0:T(8,128)} async-done(((f32[24,3072]{1,0:T(8,128)}), f32[96,3072]{1,0:T(8,128)}) %all-gather.6.cloned.1.call-update) | async-done | bytes 1179664 | tf_op jit(solution)/shard_map/all_gather | solution.py:59
  1153.6 3.9 fusion.20
  (51 shorter events, 8.3 us)
Async XLA Ops:
  6.5 1147.0 %copy-start = (f32[4,4]{1,0:T(4,128)S(1)}, f32[4,4]{1,0:T(4,128)}, u32[]{:S(2)}) copy-start(f32[4,4]{1,0:T(4,128)} %param.11) | copy-start | bytes 196
  6.5 24.6 %copy-start.9 = (s32[24,10]{0,1:T(8,128)S(1)}, s32[24,10]{0,1:T(8,128)}, u32[]{:S(2)}) copy-start(s32[24,10]{0,1:T(8,128)} %param.13) | copy-start | bytes 2884
  6.5 891.0 %all-gather.4.cloned.1.call-start = ((), (), s32[]{:S(2)}) async-start(), calls=%async_computation.4 | async-start | bytes 7925760 | tf_op jit(solution)/shard_map/all_gather | solution.py:46
  10.8 42.2 %all-to-all-start = ((f32[1,128,576]{2,0,1:T(1,128)}), f32[1,128,576]{2,0,1:T(1,128)S(1)}, u32[]{:S(2)}, u32[]{:S(2)}) async-start(f32[1,128,576]{2,0,1:T(1,128)} %copy.62), calls=%async_computation | async-start | bytes 655360 | tf_op jit(solution)/shard_map/all_to_all | solution.py:39
  906.1 9.9 copy-start.1
  908.5 22.7 %all-to-all-start.1 = ((f32[1,128,576]{2,0,1:T(1,128)}), f32[1,128,576]{2,0,1:T(1,128)}, u32[]{:S(2)}, u32[]{:S(2)}) async-start(f32[1,128,576]{2,0,1:T(1,128)} %copy.69), calls=%async_computation.1 | async-start | bytes 655360 | tf_op jit(solution)/shard_map/all_to_all | solution.py:39
  927.0 6.8 copy-start.5
  927.0 6.8 copy-start.7
  934.6 0.7 copy-start.2
  975.9 10.9 copy-start.6
  978.4 23.7 %all-to-all-start.3 = ((f32[1,128,576]{2,0,1:T(1,128)}), f32[1,128,576]{2,0,1:T(1,128)}, u32[]{:S(2)}, u32[]{:S(2)}) async-start(f32[1,128,576]{2,0,1:T(1,128)} %copy.84), calls=%async_computation.3 | async-start | bytes 655360 | tf_op jit(solution)/shard_map/all_to_all | solution.py:39
  986.5 167.0 %all-gather.6.cloned.1.call-start = ((), (), s32[]{:S(2)}) async-start(), calls=%async_computation.5 | async-start | bytes 1474560 | tf_op jit(solution)/shard_map/all_gather | solution.py:59
  997.1 7.4 copy-start.3
  997.1 7.4 copy-start.4
  997.1 7.4 copy-start.8
Sparse Core Ops, SparseCore 0:
  9.4 888.0 all-gather.3
  1005.5 148.0 all-gather.5
where the time goes:
time: 1170 us
  waiting for transfers between devices  1020 us (87%)
  matrix products  39.5 us (3%)
  starting transfers between devices  36.2 us (3%)
  blocking collectives  27.6 us (2%)
  local copies, waits for them, and re-layouts  24.4 us (2%)
  between operations  14.3 us (1%)
    all_gather x1, waiting for transfers between devices, shards(): operator_blocks = lax.all_gather(string_blocks, 'col', axis=0, tiled=True)  842 us
    all_gather x1, waiting for transfers between devices, shards(): all_roots = lax.all_gather(second[None], 'root', axis=0, tiled=True)  148 us
    all_to_all x3, starting transfers between devices, swap_layout(): lax.all_to_all(layout_pieces(stacked), 'col', split_axis=1, concat_axis=1...  35.9 us
    dot_general x4, matrix products, apply_blocks(): jnp.einsum('rifk,ifjk->rij', picked, tiles, precision=lax.Precision.HIGHEST)  35.6 us
    all_to_all x3, waiting for transfers between devices, swap_layout(): lax.all_to_all(layout_pieces(stacked), 'col', split_axis=1, concat_axis=1...  30.6 us
    all_to_all x1, blocking collectives, swap_layout(): lax.all_to_all(layout_pieces(stacked), 'col', split_axis=1, concat_axis=1...  27.6 us
  transfers between devices with their start and end apart: 5, of which 5 were waited for; matrix products, arithmetic and copies ran while one was open for 2% of the time, Pallas kernels for 0%

commit v1 on v0

--- a/solution.py
+++ b/solution.py
@@ -1,7 +1,222 @@
+import functools
+
 import jax
 import jax.numpy as jnp
 from jax import lax
+from jax.experimental import pallas as pl
+from jax.experimental.pallas import tpu as pltpu
+from jax.sharding import Mesh
 from jax.sharding import PartitionSpec as P
+
+ROOT = ("zh", "core")
+COL = ("zl", "y", "x")
+CUT = 128
+
+
+def place(**moved):
+    z = lax.axis_index("zh") * 8 + lax.axis_index("zl")
+    z = lax.rem(z + moved.get("z", 0) + 16, 16)
+    return {
+        "zh": z // 8,
+        "core": lax.rem(lax.axis_index("core") + moved.get("core", 0), 2),
+        "zl": lax.rem(z, 8),
+        "y": lax.rem(lax.axis_index("y") + moved.get("y", 0) + 4, 4),
+        "x": lax.rem(lax.axis_index("x") + moved.get("x", 0) + 4, 4),
+    }
+
+
+def gather_kernel(mine_ref, full_ref, send_sems, recv_sems, local_sem):
+    core = lax.axis_index("core")
+    here = place()
+    barrier = pltpu.get_barrier_semaphore()
+    peers = [{"z": d} for d in (1, 2, 3, 4, -1, -2, -3, -4)]
+    peers += [{"y": 1}, {"y": -1}, {"x": 1}, {"x": -1}, {"core": 1}]
+    for step in peers:
+        pl.semaphore_signal(barrier, inc=1, device_id=place(**step), device_id_type=pl.DeviceIdType.MESH)
+
+    pl.semaphore_wait(barrier, len(peers))
+
+    def spread(color):
+        rows = pl.ds(0, CUT) if color == 0 else pl.ds(CUT, 240 - CUT)
+        other_rows = pl.ds(CUT, 240 - CUT) if color == 0 else pl.ds(0, CUT)
+        first, second = ("y", "x") if color == 0 else ("x", "y")
+        pending = []
+        counter = [0]
+
+        def part(zl, a, b, rows_=None, swap=False):
+            rows_ = rows if rows_ is None else rows_
+            a_first = (first == "y") != swap
+            y, x = (a, b) if a_first else (b, a)
+            return full_ref.at[zl, y, x, rows_]
+
+        def at(step):
+            return lax.rem(here[first] + step + 4, 4)
+
+        def bt(step):
+            return lax.rem(here[second] + step + 4, 4)
+
+        def exchange(mine, theirs, to):
+            k = counter[0]
+            counter[0] += 1
+            copy = pltpu.make_async_remote_copy(
+                src_ref=mine, dst_ref=mine, send_sem=send_sems.at[k], recv_sem=recv_sems.at[k],
+                device_id=place(**to), device_id_type=pl.DeviceIdType.MESH)
+            copy.start()
+            pending.append(copy)
+            landing = pltpu.make_async_remote_copy(
+                src_ref=theirs, dst_ref=theirs, send_sem=send_sems.at[k], recv_sem=recv_sems.at[k],
+                device_id=place(**to), device_id_type=pl.DeviceIdType.MESH)
+            return landing.wait_recv
+
+        every = pl.ds(0, 8)
+        halves = (pl.ds(0, 4), pl.ds(4, 4))
+        own = pltpu.make_async_copy(mine_ref.at[rows], part(here["zl"], here[first], here[second]), local_sem)
+        own.start()
+        own.wait()
+
+        waits = []
+        for d in (1, -1, 2, -2, 3, -3, 4):
+            zl_from = lax.rem(here["zl"] - d + 8, 8)
+            waits.append(exchange(part(here["zl"], here[first], here[second]),
+                                  part(zl_from, here[first], here[second]), {"z": d}))
+        for wait in waits:
+            wait()
+
+        sibling = []
+
+        def to_sibling(zl, a, b):
+            k = counter[0]
+            counter[0] += 1
+            copy = pltpu.make_async_remote_copy(
+                src_ref=part(zl, a, b), dst_ref=part(zl, a, b), send_sem=send_sems.at[k], recv_sem=recv_sems.at[k],
+                device_id=place(core=1), device_id_type=pl.DeviceIdType.MESH)
+            copy.start()
+            pending.append(copy)
+
+        def from_sibling(zl, a, b):
+            k = counter[0]
+            counter[0] += 1
+            ref = part(zl, a, b, other_rows, True)
+            sibling.append(pltpu.make_async_remote_copy(
+                src_ref=ref, dst_ref=ref, send_sem=send_sems.at[k], recv_sem=recv_sems.at[k],
+                device_id=place(core=1), device_id_type=pl.DeviceIdType.MESH))
+
+        a0, b0 = at(0), bt(0)
+        first_waits = {}
+        first_waits[1] = exchange(part(every, a0, b0), part(every, at(-1), b0), {first: 1})
+        first_waits[-1] = exchange(part(every, a0, b0), part(every, at(1), b0), {first: -1})
+        second_waits = []
+
+        def along_second(zl, step, down, up):
+            wait_up = exchange(part(zl, at(step), b0), part(zl, at(step), bt(-1)), {second: 1})
+            wait_down = exchange(part(zl, at(step), b0), part(zl, at(step), bt(1)), {second: -1})
+            second_waits.append((step, zl, down, up, wait_up, wait_down))
+
+        along_second(every, 0, *halves)
+        to_log = [(every, 0, 0)]
+        to_sibling(every, a0, b0)
+        first_waits[1]()
+        far_low = exchange(part(halves[0], at(-1), b0), part(halves[0], at(-2), b0), {first: 1})
+        along_second(every, -1, *halves)
+        to_sibling(every, at(-1), b0)
+        first_waits[-1]()
+        far_high = exchange(part(halves[1], at(1), b0), part(halves[1], at(2), b0), {first: -1})
+        along_second(every, 1, *halves)
+        to_sibling(every, at(1), b0)
+        quarters = (pl.ds(0, 2), pl.ds(2, 2), pl.ds(4, 2), pl.ds(6, 2))
+        far_low()
+        along_second(halves[0], 2, quarters[0], quarters[1])
+        to_sibling(halves[0], at(2), b0)
+        far_high()
+        along_second(halves[1], 2, quarters[2], quarters[3])
+        to_sibling(halves[1], at(2), b0)
+
+        last = []
+        for step, zl, low, high, wait_up, wait_down in second_waits:
+            wait_up()
+            last.append((step, low, exchange(part(low, at(step), bt(-1)), part(low, at(step), bt(-2)), {second: 1})))
+            to_sibling(zl, at(step), bt(-1))
+            wait_down()
+            last.append((step, high, exchange(part(high, at(step), bt(1)), part(high, at(step), bt(2)), {second: -1})))
+            to_sibling(zl, at(step), bt(1))
+        for step, zl, wait in last:
+            wait()
+            to_sibling(zl, at(step), bt(2))
+
+        for copy in pending:
+            copy.wait_send()
+        sends = counter[0]
+        return sends
+
+    def sibling_waits(color):
+        rows = pl.ds(CUT, 240 - CUT) if color == 0 else pl.ds(0, CUT)
+        first, second = ("x", "y") if color == 0 else ("y", "x")
+
+        def at(step):
+            return lax.rem(here[first] + step + 4, 4)
+
+        def bt(step):
+            return lax.rem(here[second] + step + 4, 4)
+
+        def wait(k, zl, a, b):
+            y, x = (a, b) if first == "y" else (b, a)
+            ref = full_ref.at[zl, y, x, rows]
+            pltpu.make_async_remote_copy(
+                src_ref=ref, dst_ref=ref, send_sem=send_sems.at[k], recv_sem=recv_sems.at[k],
+                device_id=place(core=1), device_id_type=pl.DeviceIdType.MESH).wait_recv()
+
+        return wait, at, bt
+
+    for color in (0, 1):
+        @pl.when(core == color)
+        def _():
+            spread(color)
+            wait, at, bt = sibling_waits(color)
+            e = pl.ds(0, 8)
+            h = (pl.ds(0, 4), pl.ds(4, 4))
+            q = (pl.ds(0, 2), pl.ds(2, 2), pl.ds(4, 2), pl.ds(6, 2))
+            k = 7
+            k += 2
+            k += 2
+            wait(k, e, at(0), bt(0)); k += 1
+            k += 3
+            wait(k, e, at(-1), bt(0)); k += 1
+            k += 3
+            wait(k, e, at(1), bt(0)); k += 1
+            k += 2
+            wait(k, h[0], at(2), bt(0)); k += 1
+            k += 2
+            wait(k, h[1], at(2), bt(0)); k += 1
+            sets = [(0, e, h[0], h[1]), (-1, e, h[0], h[1]), (1, e, h[0], h[1]),
+                    (2, h[0], q[0], q[1]), (2, h[1], q[2], q[3])]
+            for step, zl, low, high in sets:
+                k += 1
+                wait(k, zl, at(step), bt(-1)); k += 1
+                k += 1
+                wait(k, zl, at(step), bt(1)); k += 1
+            for step, zl, low, high in sets:
+                wait(k, low, at(step), bt(2)); k += 1
+                wait(k, high, at(step), bt(2)); k += 1
+
+
+MESSAGES = 64
+
+
+def gather_operator(string_blocks):
+    full = pl.pallas_call(
+        gather_kernel,
+        out_shape=jax.ShapeDtypeStruct((8, 4, 4, 240, 128), jnp.bfloat16),
+        in_specs=[pl.BlockSpec(memory_space=pl.ANY)],
+        out_specs=pl.BlockSpec(memory_space=pl.ANY),
+        scratch_shapes=[
+            pltpu.SemaphoreType.DMA((MESSAGES,)),
+            pltpu.SemaphoreType.DMA((MESSAGES,)),
+            pltpu.SemaphoreType.DMA,
+        ],
+        compiler_params=pltpu.CompilerParams(collective_id=0, has_side_effects=True),
+        name="gather_operator",
+    )(string_blocks)
+    return full.reshape(30720, 128)
 
 
 def apply_blocks(matrix, operator_blocks, block_cols):
@@ -36,14 +251,14 @@
 
 
 def swap_layout(stacked):
-    moved = lax.all_to_all(layout_pieces(stacked), "col", split_axis=1, concat_axis=1, tiled=True)
+    moved = lax.all_to_all(layout_pieces(stacked), COL, split_axis=1, concat_axis=1, tiled=True)
     return layout_whole(moved, stacked.shape[1])
 
 
 def shards(coeffs, diagonal, shift, rotation, string_blocks, block_cols):
     start = coeffs[0]
     energy = shift[0]
-    operator_blocks = lax.all_gather(string_blocks, "col", axis=0, tiled=True)
+    operator_blocks = gather_operator(string_blocks)
 
     def apply_local(matrix):
         return apply_blocks(matrix, operator_blocks, block_cols)
@@ -56,17 +271,19 @@
 
     first = 0.5 * (sigma_local(start) - energy * start)
     second = sigma_local(first) - energy * first - start
-    all_roots = lax.all_gather(second[None], "root", axis=0, tiled=True)
-    weights = lax.dynamic_index_in_dim(rotation, lax.axis_index("root"), 0, keepdims=False)
+    all_roots = lax.all_gather(second[None], ROOT, axis=0, tiled=True)
+    root = lax.axis_index("zh") * 2 + lax.axis_index("core")
+    weights = lax.dynamic_index_in_dim(rotation, root, 0, keepdims=False)
     result = jnp.einsum("s,sba->ba", weights, all_roots, precision=lax.Precision.HIGHEST)
     return result[None]
 
 
 def solution(mesh):
+    split = Mesh(mesh.devices.reshape(2, 2, 8, 4, 4), ROOT + COL)
     return jax.shard_map(
         shards,
-        mesh=mesh,
-        in_specs=(P("root", "col", None), P("col", None), P("root"), P(), P("col", None), P()),
-        out_specs=P("root", "col", None),
+        mesh=split,
+        in_specs=(P(ROOT, COL, None), P(COL, None), P(ROOT), P(), P(COL, None), P()),
+        out_specs=P(ROOT, COL, None),
         check_vma=False,
     )

time: 1170 us -> 277 us (0.24)
  waiting for transfers between devices: 1020 us -> 72.5 us
  Pallas kernels: 0 us -> 52.4 us
    all_gather x2 -> x1, waiting for transfers between devices: 990 us -> 51.5 us  [shards(): all_roots = lax.all_gather(second[None], ROOT, axis=0, tiled=True)]
    pallas_call x0 -> x1, Pallas kernels: none -> 52.4 us  [gather_operator(): pl.pallas_call(gather_kernel, out_shape=jax.ShapeDtypeStruct((8, 4, 4, 24...]
  transfers between devices with their start and end apart: 5 -> 4, of which waited for: 5 -> 3; matrix products, arithmetic and copies ran while one was open for 2% -> 8% of each run, Pallas kernels for 0% -> 19%
where the time goes in v1:
time: 277 us; the launch traced here: 276 us
  waiting for transfers between devices  72.5 us (26%)
  Pallas kernels  52.4 us (19%)
  starting transfers between devices  41.4 us (15%)
  matrix products  39.5 us (14%)
  blocking collectives  30.4 us (11%)
  local copies, waits for them, and re-layouts  24.3 us (9%)
  between operations  14.4 us (5%)
    pallas_call x1, Pallas kernels, gather_operator(): pl.pallas_call(gather_kernel, out_shape=jax.ShapeDtypeStruct((8, 4, 4, 24...  52.4 us
    all_gather x1, waiting for transfers between devices, shards(): all_roots = lax.all_gather(second[None], ROOT, axis=0, tiled=True)  51.5 us
    all_to_all x3, starting transfers between devices, swap_layout(): lax.all_to_all(layout_pieces(stacked), COL, split_axis=1, concat_axis=1,...  41.1 us
    dot_general x4, matrix products, apply_blocks(): jnp.einsum('rifk,ifjk->rij', picked, tiles, precision=lax.Precision.HIGHEST)  35.6 us
    all_to_all x1, blocking collectives, swap_layout(): lax.all_to_all(layout_pieces(stacked), COL, split_axis=1, concat_axis=1,...  30.4 us
    all_to_all x3, waiting for transfers between devices, swap_layout(): lax.all_to_all(layout_pieces(stacked), COL, split_axis=1, concat_axis=1,...  21 us
  transfers between devices with their start and end apart: 4, of which 3 were waited for; matrix products, arithmetic and copies ran while one was open for 8% of the time, Pallas kernels for 19%

profile of v1, /device:TPU:1, one launch (start us, length us, event | category | flops | bytes accessed | tf_op | source)
XLA Modules:
  0.0 276.5 jit_solution(14981785054242051757)
XLA Ops:
  6.5 2.1 reshape_broadcast_in_dim_squeeze.3
  9.1 0.9 copy.62
  10.0 20.4 %all-to-all-start = ((f32[1,128,576]{2,0,1:T(1,128)}), f32[1,128,576]{2,0,1:T(1,128)S(1)}, u32[]{:S(2)}, u32[]{:S(2)}) async-start(f32[1,128,576]{2,0,1:T(1,128)} %copy.62), calls=%async_computation | async-start | bytes 655360 | tf_op jit(solution)/shard_map/all_to_all | solution.py:254
  30.4 52.4 %gather_operator.1 = bf16[8,4,4,240,128]{4,3,2,1,0:T(8,128)(2,1)} custom-call(bf16[240,128]{1,0:T(8,128)(2,1)} %mine_ref.1), custom_call_target="tpu_custom_call" | custom-call | tf_op jit(solution)/shard_map/gather_operator/pallas_call | solution.py:206
  83.8 0.9 reshape_squeeze_reshape.6
  84.8 1.0 gather_fusion.1
  85.8 8.6 %fusion.25 = f32[24,24,128]{2,0,1:T(8,128)S(1)} fusion(bf16[24,10,128,128]{3,2,1,0:T(8,128)(2,1)} %bitcast.121, f32[24,10,24,128]{3,2,1,0:T(8,128)S(1)} %bitcast.128, pred[24,10]{1,0:T(8,128)(4,1)S(1)} %copy.55), kind=kOutput, calls=%fused_computation.27 | convolution fusion | flops 1133199360 | bytes 11108592 | tf_op jit(solution)/shard_map/rifk,ifjk->rij/dot_general | solution.py:229
  94.5 1.0 reshape_broadcast_in_dim_reshape.6
  95.9 0.9 copy.69
  96.9 11.6 %all-to-all-start.1 = ((f32[1,128,576]{2,0,1:T(1,128)}), f32[1,128,576]{2,0,1:T(1,128)}, u32[]{:S(2)}, u32[]{:S(2)}) async-start(f32[1,128,576]{2,0,1:T(1,128)} %copy.69), calls=%async_computation.1 | async-start | bytes 655360 | tf_op jit(solution)/shard_map/all_to_all | solution.py:254
  108.6 1.0 gather_fusion
  110.3 9.2 %fusion.22 = f32[24,3,8,128]{3,2,1,0:T(8,128)} fusion(bf16[24,10,128,128]{3,2,1,0:T(8,128)(2,1)} %bitcast.122, f32[24,10,24,128]{3,2,1,0:T(8,128)S(1)} %bitcast.127, pred[24,10]{1,0:T(8,128)(4,1)S(1)} %copy.55), kind=kOutput, calls=%fused_computation.26 | convolution fusion | flops 1133199360 | bytes 11108592 | tf_op jit(solution)/shard_map/rifk,ifjk->rij/dot_general | solution.py:229
  119.5 10.3 %all-to-all-done.1 = f32[1,128,576]{2,0,1:T(1,128)} async-done(((f32[1,128,576]{2,0,1:T(1,128)}), f32[1,128,576]{2,0,1:T(1,128)}, u32[]{:S(2)}, u32[]{:S(2)}) %all-to-all-start.1) | async-done | bytes 294944 | tf_op jit(solution)/shard_map/all_to_all | solution.py:254
  129.8 1.1 copy.70
  131.4 0.9 squeeze_reshape.6
  132.3 0.8 fusion.39
  133.8 1.1 reshape_broadcast_in_dim.3
  135.6 30.4 %all_to_all.20 = f32[1,128,576]{2,0,1:T(1,128)S(1)} all-to-all(f32[1,128,576]{2,0,1:T(1,128)S(1)} %copy.77), channel_id=1, replica_groups=mesh['zh'=2,'core'=2,'zl'=8,'y'=4,'x'=4] {'zl','y','x'}, dimensions={1} | all-to-all | bytes 589824 | tf_op jit(solution)/shard_map/all_to_all | solution.py:254
  166.6 0.9 reshape_squeeze_reshape.7
  167.6 1.0 gather_fusion.3
  168.6 8.6 %fusion.31 = f32[24,24,128]{2,0,1:T(8,128)S(1)} fusion(bf16[24,10,128,128]{3,2,1,0:T(8,128)(2,1)} %bitcast.123, f32[24,10,24,128]{3,2,1,0:T(8,128)S(1)} %bitcast.129, pred[24,10]{1,0:T(8,128)(4,1)S(1)} %copy.55), kind=kOutput, calls=%fused_computation.29 | convolution fusion | flops 1133199360 | bytes 11108592 | tf_op jit(solution)/shard_map/rifk,ifjk->rij/dot_general | solution.py:229
  177.3 1.0 reshape_broadcast_in_dim_reshape.7
  178.7 0.9 copy.84
  179.6 9.1 %all-to-all-start.3 = ((f32[1,128,576]{2,0,1:T(1,128)}), f32[1,128,576]{2,0,1:T(1,128)}, u32[]{:S(2)}, u32[]{:S(2)}) async-start(f32[1,128,576]{2,0,1:T(1,128)} %copy.84), calls=%async_computation.3 | async-start | bytes 655360 | tf_op jit(solution)/shard_map/all_to_all | solution.py:254
  189.1 1.0 gather_fusion.2
  190.1 9.2 %fusion.28 = f32[24,3,8,128]{3,2,1,0:T(8,128)} fusion(bf16[24,10,128,128]{3,2,1,0:T(8,128)(2,1)} %bitcast.124, f32[24,10,24,128]{3,2,1,0:T(8,128)S(1)} %bitcast.126, pred[24,10]{1,0:T(8,128)(4,1)S(1)} %copy.55), kind=kOutput, calls=%fused_computation.28 | convolution fusion | flops 1133199360 | bytes 11108592 | tf_op jit(solution)/shard_map/rifk,ifjk->rij/dot_general | solution.py:229
  199.3 10.7 %all-to-all-done.3 = f32[1,128,576]{2,0,1:T(1,128)} async-done(((f32[1,128,576]{2,0,1:T(1,128)}), f32[1,128,576]{2,0,1:T(1,128)}, u32[]{:S(2)}, u32[]{:S(2)}) %all-to-all-start.3) | async-done | bytes 294944 | tf_op jit(solution)/shard_map/all_to_all | solution.py:254
  210.1 1.1 copy.85
  211.7 0.9 squeeze_reshape.7
  212.6 0.8 fusion.36
  213.4 51.5 %all-gather.3.cloned.1.call-done = f32[96,3072]{1,0:T(8,128)} async-done(((f32[24,3072]{1,0:T(8,128)}), f32[96,3072]{1,0:T(8,128)}) %all-gather.3.cloned.1.call-update) | async-done | bytes 1179664 | tf_op jit(solution)/shard_map/all_gather | solution.py:274
  264.9 3.9 %fusion.20 = f32[1,24,3072]{2,0,1:T(1,128)S(1)} fusion(f32[4,24,3072]{2,1,0:T(8,128)} %bitcast.143, f32[4,4]{1,0:T(4,128)S(1)} %copy-done, s32[]{:T(128)S(6)} %select_n.11), kind=kOutput, calls=%fused_computation.24 | convolution fusion | flops 3538944 | bytes 1475076 | tf_op jit(solution)/shard_map/s,sba->ba/dot_general | solution.py:277
  (49 shorter events, 6.8 us)
Async XLA Ops:
  6.5 258.4 %copy-start = (f32[4,4]{1,0:T(4,128)S(1)}, f32[4,4]{1,0:T(4,128)}, u32[]{:S(2)}) copy-start(f32[4,4]{1,0:T(4,128)} %param.11) | copy-start | bytes 196
  10.0 73.1 %all-to-all-start = ((f32[1,128,576]{2,0,1:T(1,128)}), f32[1,128,576]{2,0,1:T(1,128)S(1)}, u32[]{:S(2)}, u32[]{:S(2)}) async-start(f32[1,128,576]{2,0,1:T(1,128)} %copy.62), calls=%async_computation | async-start | bytes 655360 | tf_op jit(solution)/shard_map/all_to_all | solution.py:254
  30.4 52.4 %copy-start.9 = (s32[24,10]{0,1:T(8,128)S(1)}, s32[24,10]{0,1:T(8,128)}, u32[]{:S(2)}) copy-start(s32[24,10]{0,1:T(8,128)} %param.13) | copy-start | bytes 2884
  94.4 14.1 %copy-start.1 = (f32[1,24,3072]{2,1,0:T(8,128)S(1)}, f32[1,24,3072]{2,1,0:T(8,128)}, u32[]{:S(2)}) copy-start(f32[1,24,3072]{2,1,0:T(8,128)} %param.8) | copy-start | bytes 884740
  96.9 32.9 %all-to-all-start.1 = ((f32[1,128,576]{2,0,1:T(1,128)}), f32[1,128,576]{2,0,1:T(1,128)}, u32[]{:S(2)}, u32[]{:S(2)}) async-start(f32[1,128,576]{2,0,1:T(1,128)} %copy.69), calls=%async_computation.1 | async-start | bytes 655360 | tf_op jit(solution)/shard_map/all_to_all | solution.py:254
  119.5 12.7 %copy-start.5 = (f32[24,3,8,128]{3,2,1,0:T(8,128)S(1)}, f32[24,3,8,128]{3,2,1,0:T(8,128)}, u32[]{:S(2)}) copy-start(f32[24,3,8,128]{3,2,1,0:T(8,128)} %fusion.22) | copy-start | bytes 884740
  119.5 12.7 %copy-start.7 = (f32[24,3072]{1,0:T(8,128)S(1)}, f32[24,3072]{1,0:T(8,128)}, u32[]{:S(2)}) copy-start(f32[24,3072]{1,0:T(8,128)} %param.9) | copy-start | bytes 884740
  133.0 0.7 copy-start.2
  177.2 11.9 %copy-start.6 = (f32[3,24,8,128]{3,2,1,0:T(8,128)S(1)}, f32[3,24,8,128]{3,2,1,0:T(8,128)}, u32[]{:S(2)}) copy-start(f32[3,24,8,128]{3,2,1,0:T(8,128)} %get-tuple-element.6) | copy-start | bytes 884740
  179.6 30.4 %all-to-all-start.3 = ((f32[1,128,576]{2,0,1:T(1,128)}), f32[1,128,576]{2,0,1:T(1,128)}, u32[]{:S(2)}, u32[]{:S(2)}) async-start(f32[1,128,576]{2,0,1:T(1,128)} %copy.84), calls=%async_computation.3 | async-start | bytes 655360 | tf_op jit(solution)/shard_map/all_to_all | solution.py:254
  188.7 76.2 %all-gather.3.cloned.1.call-start = ((), (), s32[]{:S(2)}) async-start(), calls=%async_computation.4 | async-start | bytes 1474560 | tf_op jit(solution)/shard_map/all_gather | solution.py:274
  199.3 13.2 %copy-start.3 = (f32[24,3072]{1,0:T(8,128)S(1)}, f32[24,3072]{1,0:T(8,128)}, u32[]{:S(2)}) copy-start(f32[24,3072]{1,0:T(8,128)} %copy-done.2) | copy-start | bytes 884740
  199.3 13.2 %copy-start.4 = (f32[24,3,8,128]{3,2,1,0:T(8,128)S(1)}, f32[24,3,8,128]{3,2,1,0:T(8,128)}, u32[]{:S(2)}) copy-start(f32[24,3,8,128]{3,2,1,0:T(8,128)} %fusion.28) | copy-start | bytes 884740
  199.3 13.2 %copy-start.8 = (f32[24,3072]{1,0:T(8,128)S(1)}, f32[24,3072]{1,0:T(8,128)}, u32[]{:S(2)}) copy-start(f32[24,3072]{1,0:T(8,128)} %param.9) | copy-start | bytes 884740
Sparse Core Ops, SparseCore 0:
  213.5 51.3 all-gather.2

commit v2 on v0

v2 whole, which is shorter than its diff:
```python
import jax
import jax.numpy as jnp
from jax import lax
from jax.experimental import pallas as pl
from jax.experimental.pallas import tpu as pltpu
from jax.sharding import Mesh
from jax.sharding import PartitionSpec as P

ROOT = ("zh", "core")
COL = ("zl", "y", "x")
CUT = 128
F32, BF16 = jnp.float32, jnp.bfloat16
ONTO = pl.DeviceIdType.MESH

E, H, Q = (0, 8), ((0, 4), (4, 4)), ((0, 2), (2, 2), (4, 2), (6, 2))
Z_STEPS = (1, -1, 2, -2, 3, -3, 4)


def spread_plan():
    plan = [("z", ("z", d), None) for d in Z_STEPS]

    def both(zs, a):
        plan.append(((zs, a, 0), ("second", 1), (zs, a, -1)))
        plan.append(((zs, a, 0), ("second", -1), (zs, a, 1)))

    def sibling(zs, a, b):
        plan.append(((zs, a, b), ("core", 1), "sibling"))

    plan.append(((E, 0, 0), ("first", 1), (E, -1, 0)))
    plan.append(((E, 0, 0), ("first", -1), (E, 1, 0)))
    both(E, 0)
    sibling(E, 0, 0)
    marks = {"start": (7, 12)}
    steps = []
    n = len(plan)
    plan.append(((H[0], -1, 0), ("first", 1), (H[0], -2, 0)))
    both(E, -1)
    sibling(E, -1, 0)
    steps.append((7, (n, len(plan))))
    far_low = n
    n = len(plan)
    plan.append(((H[1], 1, 0), ("first", -1), (H[1], 2, 0)))
    both(E, 1)
    sibling(E, 1, 0)
    steps.append((8, (n, len(plan))))
    far_high = n
    n = len(plan)
    both(H[0], 2)
    sibling(H[0], 2, 0)
    steps.append((far_low, (n, len(plan))))
    n = len(plan)
    both(H[1], 2)
    sibling(H[1], 2, 0)
    steps.append((far_high, (n, len(plan))))
    sets = [(0, E, H[0], H[1], 9), (-1, E, H[0], H[1], 13), (1, E, H[0], H[1], 17),
            (2, H[0], Q[0], Q[1], 20), (2, H[1], Q[2], Q[3], 23)]
    last = []
    for a, zs, low, high, number in sets:
        n = len(plan)
        plan.append(((low, a, -1), ("second", 1), (low, a, -2)))
        sibling(zs, a, -1)
        steps.append((number, (n, len(plan))))
        last.append((n, low, a))
        n = len(plan)
        plan.append(((high, a, 1), ("second", -1), (high, a, 2)))
        sibling(zs, a, 1)
        steps.append((number + 1, (n, len(plan))))
        last.append((n, high, a))
    for number, zs, a in last:
        n = len(plan)
        sibling(zs, a, 2)
        steps.append((number, (n, len(plan))))
    return plan, marks, steps


PLAN, MARKS, STEPS = spread_plan()


def device(z, y, x, core):
    return {"zh": z // 8, "core": core, "zl": lax.rem(z, 8), "y": y, "x": x}


def split(value):
    high = value.astype(BF16).astype(F32)
    return jnp.concatenate([high, value - high], axis=0).astype(BF16)


def kernel(v_ref, diag_ref, shift_ref, rot_ref, mine_ref, cols_ref, out_ref,
           op, grid_v, grid_t, turn, zs_v, zs_t, zs_f, zs_g, zb_v, zb_t, zb_f, zb_g,
           xb, vc, rv, tb, fm, fsib, pm, psib, fr, pr, wf, wg, ib_f, ib_g, hf, eb,
           op_send, op_recv, op_local, plane_send, plane_recv, z_send, z_recv, pair_send, pair_recv):
    zh, core, zl = lax.axis_index("zh"), lax.axis_index("core"), lax.axis_index("zl")
    y, x = lax.axis_index("y"), lax.axis_index("x")
    z = zh * 8 + zl
    p = y * 4 + x

    def at_z(other):
        return device(other, y, x, core)

    def at_p(other):
        return {"zh": zh, "core": core, "zl": zl, "y": other // 4, "x": lax.rem(other, 4)}

    pair = {"zh": zh, "core": 1 - core, "zl": zl, "y": y, "x": x}

    energy = shift_ref[0]
    eb[zh] = jnp.full((8, 128), energy, F32)
    turn[...] = jnp.zeros_like(turn)
    barrier = pltpu.get_barrier_semaphore()

    @pl.loop(1, 16)
    def _(step):
        pl.semaphore_signal(barrier, inc=1, device_id=at_z(lax.rem(z + step, 16)), device_id_type=ONTO)
        pl.semaphore_signal(barrier, inc=1, device_id=at_p(lax.rem(p + step, 16)), device_id_type=ONTO)

    pl.semaphore_signal(barrier, inc=1, device_id=pair, device_id_type=ONTO)
    pl.semaphore_wait(barrier, 31)

    def plane_copy(kind, src, dst, to, source):
        return pltpu.make_async_remote_copy(
            src_ref=src, dst_ref=dst, send_sem=plane_send.at[kind, to], recv_sem=plane_recv.at[kind, source],
            device_id=at_p(to), device_id_type=ONTO)

    def z_copy(kind, src, dst, to, source):
        return pltpu.make_async_remote_copy(
            src_ref=src, dst_ref=dst, send_sem=z_send.at[kind, to], recv_sem=z_recv.at[kind, source],
            device_id=at_z(to), device_id_type=ONTO)

    def rows24(ref, index):
        return ref.at[pl.ds(pl.multiple_of(index * 24, 8), 24), :]

    def wait_plane(kind, slot):
        @pl.loop(1, 16)
        def _(step):
            other = lax.rem(p + step, 16)
            plane_copy(kind, slot(other), slot(other), other, other).wait_recv()

    def wait_z(kind, ref):
        @pl.loop(1, 16)
        def _(step):
            other = lax.rem(z + step, 16)
            z_copy(kind, ref.at[other], ref.at[other], other, other).wait_recv()

    def sent_plane(kind, slot):
        @pl.loop(1, 16)
        def _(step):
            other = lax.rem(p + step, 16)
            plane_copy(kind, slot(other), slot(other), other, other).wait_send()

    def sent_z(kind, ref):
        @pl.loop(1, 16)
        def _(step):
            other = lax.rem(z + step, 16)
            z_copy(kind, ref.at[other], ref.at[other], other, other).wait_send()

    def spread(color):
        rows = (0, CUT) if color == 0 else (CUT, 240 - CUT)
        others = (CUT, 240 - CUT) if color == 0 else (0, CUT)
        place = {"y": y, "x": x}

        def of(piece, part, first, second):
            zs, a, b = piece
            index = {first: lax.rem(place[first] + a + 4, 4), second: lax.rem(place[second] + b + 4, 4)}
            return op.at[pl.ds(zs[0], zs[1]), index["y"], index["x"], pl.ds(part[0], part[1])]

        first, second = ("y", "x") if color == 0 else ("x", "y")

        def copy(number, landing=False):
            piece, (axis, step), lands = PLAN[number]
            if piece == "z":
                source = lax.rem(zl - step + 8, 8) if landing else zl
                ref = op.at[source, y, x, pl.ds(rows[0], rows[1])]
                to = at_z(lax.rem(z + step + 16, 16))
            elif axis == "core":
                ref = of(piece, others, second, first) if landing else of(piece, rows, first, second)
                to = pair
            else:
                ref = of(lands if landing else piece, rows, first, second)
                name = first if axis == "first" else second
                there = dict(place)
                there[name] = lax.rem(place[name] + step + 4, 4)
                to = device(z, there["y"], there["x"], core)
            return pltpu.make_async_remote_copy(
                src_ref=ref, dst_ref=ref, send_sem=op_send.at[number], recv_sem=op_recv.at[number],
                device_id=to, device_id_type=ONTO)

        return rows, copy

    def by_color(body):
        for color in (0, 1):
            @pl.when(core == color)
            def _():
                body(*spread(color))

    def spread_start(rows, copy):
        part = pl.ds(rows[0], rows[1])
        own = pltpu.make_async_copy(mine_ref.at[part], op.at[zl, y, x, part], op_local)
        own.start()
        own.wait()
        for number in range(7):
            copy(number).start()

    def spread_on(rows, copy):
        for number in range(7):
            copy(number, True).wait_recv()
        for number in range(*MARKS["start"]):
            copy(number).start()

    def spread_rest(rows, copy):
        for number, (low, high) in STEPS:
            copy(number, True).wait_recv()
            for follow in range(low, high):
                copy(follow).start()
        for number in range(len(PLAN)):
            if PLAN[number][1][0] == "core":
                copy(number, True).wait_recv()

    def spread_sent(rows, copy):
        for number in range(len(PLAN)):
            copy(number).wait_send()

    def window(target):
        return pl.ds(pl.multiple_of((3 * (target // 2) + lax.rem(target, 2)) * 128, 128), 256)

    half = pl.ds(pl.multiple_of(lax.rem(p, 2) * 64, 64), 192)
    mine24 = pl.ds(pl.multiple_of(p * 24, 8), 24)

    def turn_rows(grid, zs):
        for k in range(3):
            rows = slice(128 * k, 128 * k + 128)
            turn[0:128, :] = grid[rows, 0:128].T
            turn[128:256, :] = grid[rows, 128:256].T
            columns = turn[half, :]
            for target in range(16):
                zs[target, 12 * k:12 * k + 12, :] = columns[12 * target:12 * target + 12]

    def send_z(kind, zs, zb, target):
        @pl.when(target != z)
        def _():
            z_copy(kind, zs.at[target], zb.at[z], target, z).start()

        @pl.when(target == z)
        def _():
            zb[z] = zs[z]

    def send_all_z(kind, zs, zb):
        @pl.loop(0, 16)
        def _(step):
            send_z(kind, zs, zb, lax.rem(z + 8 + step, 16))

    def turn_columns(zb, rows_out):
        for k in range(3):
            turn[half, :] = jnp.concatenate([zb[source, 12 * k:12 * k + 12, :] for source in range(16)], axis=0)
            rows = slice(128 * k, 128 * k + 128)
            rows_out[rows, 0:128] = turn[0:128, :].T
            rows_out[rows, 128:256] = turn[128:256, :].T

    def send_rows(kind, rows_out, ib):
        @pl.loop(1, 16)
        def _(step):
            target = lax.rem(p + step, 16)
            plane_copy(kind, rows24(rows_out, target), ib.at[p], target, p).start()

        ib[p] = rows_out[mine24, :]

    low_lanes = lax.broadcasted_iota(jnp.int32, (24, 128), 1) < 64

    def merged(ib, m):
        even, odd = ib[2 * m], ib[2 * m + 1]
        return even[:, 0:128], jnp.where(low_lanes, even[:, 128:256], odd[:, 0:128]), odd[:, 128:256]

    def block(m, ii, f):
        row = ii * 1280 + f * 128
        parts, left = [], 128
        while left:
            place, offset = divmod(row, 240)
            take = min(left, 240 - offset)
            parts.append(op[m, place // 4, place % 4, offset:offset + take, :])
            row, left = row + take, left - take
        return parts[0] if len(parts) == 1 else jnp.concatenate(parts, axis=0)

    def operate(first, emit, after=None):
        @pl.loop(0, 8)
        def _(step):
            m = lax.rem(first + step, 8)
            for ii in range(3):
                vectors = jnp.concatenate([xb[cols_ref[3 * m + ii, f]] for f in range(10)], axis=1)
                blocks = jnp.concatenate([block(m, ii, f) for f in range(10)], axis=1)
                both = lax.dot_general(vectors, blocks, (((1,), (1,)), ((), ())), preferred_element_type=F32)
                emit(m, ii, both[0:24] + both[24:48])
            if after is not None:
                after(m)

    def lanes(m, ii):
        return pl.ds(pl.multiple_of((3 * m + ii) * 128, 128), 128)

    @pl.loop(1, 16)
    def _(step):
        target = lax.rem(p + step, 16)
        plane_copy(0, v_ref.at[:, window(target)], grid_v.at[mine24, :], target, p).start()

    grid_v[mine24, :] = v_ref[:, window(p)]
    by_color(spread_start)
    energy_copy = pltpu.make_async_remote_copy(
        src_ref=eb.at[zh], dst_ref=eb.at[zh], send_sem=pair_send.at[2], recv_sem=pair_recv.at[2],
        device_id=at_z(lax.rem(z + 8, 16)), device_id_type=ONTO)
    energy_copy.start()

    @pl.loop(0, 8)
    def _(m):
        for ii in range(3):
            xb[3 * m + ii] = split(v_ref[:, lanes(m, ii)])

    by_color(spread_on)
    wait_plane(0, lambda other: rows24(grid_v, other))
    turn_rows(grid_v, zs_v)
    send_all_z(0, zs_v, zb_v)
    by_color(spread_rest)

    def emit_t(m, ii, value):
        here = lanes(m, ii)
        tb[m, :, 128 * ii:128 * ii + 128] = value + (diag_ref[:, here] - energy) * v_ref[:, here]

    def after_t(m):
        for odd in (0, 1):
            target = 2 * m + odd
            part = tb.at[m, :, pl.ds(128 * odd, 256)]

            @pl.when(target != p)
            def _():
                plane_copy(1, part, grid_t.at[mine24, :], target, p).start()

            @pl.when(target == p)
            def _():
                grid_t[mine24, :] = tb[m, :, 128 * odd:128 * odd + 256]

    operate(lax.rem(p // 2 + 1, 8), emit_t, after_t)

    wait_plane(1, lambda other: rows24(grid_t, other))
    turn_rows(grid_t, zs_t)
    send_all_z(1, zs_t, zb_t)

    wait_z(0, zb_v)

    @pl.loop(0, 8)
    def _(m):
        for k in range(3):
            part = slice(12 * k, 12 * k + 12)
            both = jnp.concatenate([zb_v[m, part, :], zb_v[8 + m, part, :]], axis=0)
            vc[3 * m + k] = both
            xb[3 * m + k] = split(both)

    def emit_rv(m, ii, value):
        rv[3 * m + ii] = value

    operate(0, emit_rv)
    wait_z(1, zb_t)

    other_energy = pltpu.make_async_remote_copy(
        src_ref=eb.at[1 - zh], dst_ref=eb.at[1 - zh], send_sem=pair_send.at[2], recv_sem=pair_recv.at[2],
        device_id=at_z(lax.rem(z + 8, 16)), device_id_type=ONTO)
    other_energy.wait_recv()
    upper = lax.broadcasted_iota(jnp.int32, (24, 128), 0) < 12
    shifts = jnp.where(upper, jnp.broadcast_to(eb[0, 0:1, :], (24, 128)), jnp.broadcast_to(eb[1, 0:1, :], (24, 128)))

    def weights(to_core):
        straight = jnp.where(upper, rot_ref[to_core, core], rot_ref[2 + to_core, 2 + core])
        crossed = jnp.where(upper, rot_ref[to_core, 2 + core], rot_ref[2 + to_core, core])
        return straight, crossed

    here_straight, here_crossed = weights(core)
    there_straight, there_crossed = weights(1 - core)

    def swapped(value):
        return jnp.concatenate([value[12:24], value[0:12]], axis=0)

    @pl.loop(0, 8)
    def _(m):
        for k in range(3):
            c = 3 * m + k
            part = slice(12 * k, 12 * k + 12)
            t = jnp.concatenate([zb_t[m, part, :], zb_t[8 + m, part, :]], axis=0)
            first = 0.5 * (rv[c] + t)
            turned = swapped(first)
            rest = shifts * first + vc[c]
            rest_turned = swapped(rest)
            fm[c] = here_straight * first + here_crossed * turned
            fsib[c] = there_straight * first + there_crossed * turned
            pm[c] = here_straight * rest + here_crossed * rest_turned
            psib[c] = there_straight * rest + there_crossed * rest_turned

    def pair_copy(index, src, dst):
        return pltpu.make_async_remote_copy(
            src_ref=src, dst_ref=dst, send_sem=pair_send.at[index], recv_sem=pair_recv.at[index],
            device_id=pair, device_id_type=ONTO)

    pair_copy(0, fsib, fr).start()
    pair_copy(1, psib, pr).start()
    pair_copy(0, fsib, fr).wait_recv()

    @pl.loop(0, 8)
    def _(step):
        m = lax.rem(zl + step, 8)
        for k in range(3):
            c = 3 * m + k
            value = fm[c] + fr[c]
            xb[c] = split(value)
            zs_f[m, 12 * k:12 * k + 12, :] = value[0:12]
            zs_f[8 + m, 12 * k:12 * k + 12, :] = value[12:24]
        send_z(2, zs_f, zb_f, m)
        send_z(2, zs_f, zb_f, m + 8)

    pair_copy(1, psib, pr).wait_recv()

    def emit_g(m, ii, value):
        c = 3 * m + ii
        g = value - (pm[c] + pr[c])
        zs_g[m, 12 * ii:12 * ii + 12, :] = g[0:12]
        zs_g[8 + m, 12 * ii:12 * ii + 12, :] = g[12:24]

    def after_g(m):
        send_z(3, zs_g, zb_g, m)
        send_z(3, zs_g, zb_g, m + 8)

    operate(zl, emit_g, after_g)

    wait_z(2, zb_f)
    turn_columns(zb_f, wf)
    send_rows(2, wf, ib_f)
    wait_plane(2, lambda other: ib_f.at[other])

    @pl.loop(0, 8)
    def _(m):
        for ii, tile in enumerate(merged(ib_f, m)):
            hf[m, :, 128 * ii:128 * ii + 128] = tile
            xb[3 * m + ii] = split(tile)

    def emit_out(m, ii, value):
        here = lanes(m, ii)
        out_ref[:, here] = value + diag_ref[:, here] * hf[m, :, 128 * ii:128 * ii + 128]

    operate(0, emit_out)
    wait_z(3, zb_g)
    turn_columns(zb_g, wg)
    send_rows(3, wg, ib_g)
    wait_plane(3, lambda other: ib_g.at[other])

    @pl.loop(0, 8)
    def _(m):
        for ii, tile in enumerate(merged(ib_g, m)):
            here = lanes(m, ii)
            out_ref[:, here] = out_ref[:, here] + tile

    by_color(spread_sent)
    energy_copy.wait_send()
    pair_copy(0, fsib, fr).wait_send()
    pair_copy(1, psib, pr).wait_send()
    sent_plane(0, lambda other: rows24(grid_v, other))
    sent_plane(1, lambda other: rows24(grid_t, other))
    sent_plane(2, lambda other: ib_f.at[other])
    sent_plane(3, lambda other: ib_g.at[other])
    for kind, ref in enumerate((zs_v, zs_t, zs_f, zs_g)):
        sent_z(kind, ref)


def shards(coeffs, diagonal, shift, rotation, string_blocks, block_cols):
    vmem = pl.BlockSpec(memory_space=pltpu.VMEM)
    smem = pl.BlockSpec(memory_space=pltpu.SMEM)
    grid = pltpu.VMEM((384, 256), F32)
    packed = pltpu.VMEM((16, 36, 128), F32)
    chunks = pltpu.VMEM((24, 24, 128), F32)
    windows = pltpu.VMEM((16, 24, 256), F32)
    wide = pltpu.VMEM((8, 24, 384), F32)
    dma = pltpu.SemaphoreType.DMA
    result = pl.pallas_call(
        kernel,
        out_shape=jax.ShapeDtypeStruct((24, 3072), F32),
        in_specs=[vmem, vmem, smem, smem, vmem, smem],
        out_specs=vmem,
        scratch_shapes=[
            pltpu.VMEM((8, 4, 4, 240, 128), BF16),
            grid, grid, pltpu.VMEM((256, 128), F32),
            packed, packed, packed, packed, packed, packed, packed, packed,
            pltpu.VMEM((24, 48, 128), BF16),
            chunks, chunks, wide,
            chunks, chunks, chunks, chunks, chunks, chunks,
            grid, grid, windows, windows, wide,
            pltpu.VMEM((2, 8, 128), F32),
            dma((len(PLAN),)), dma((len(PLAN),)), dma,
            dma((4, 16)), dma((4, 16)), dma((4, 16)), dma((4, 16)), dma((3,)), dma((3,)),
        ],
        compiler_params=pltpu.CompilerParams(
            collective_id=0, has_side_effects=True, vmem_limit_bytes=48 * 1024 * 1024),
        name="filter",
    )(coeffs[0], diagonal, shift, rotation, string_blocks, block_cols)
    return result[None]


def solution(mesh):
    split_mesh = Mesh(mesh.devices.reshape(2, 2, 8, 4, 4), ROOT + COL)
    return jax.shard_map(
        shards,
        mesh=split_mesh,
        in_specs=(P(ROOT, COL, None), P(COL, None), P(ROOT), P(), P(COL, None), P()),
        out_specs=P(ROOT, COL, None),
        check_vma=False,
    )
```

time: 1170 us -> 129 us (0.11)
  waiting for transfers between devices: 1020 us -> 0 us
  Pallas kernels: 0 us -> 124 us
  matrix products: 39.5 us -> 0 us
  starting transfers between devices: 36.2 us -> 0 us
  blocking collectives: 27.6 us -> 0 us
  local copies, waits for them, and re-layouts: 24.4 us -> 4.25 us
  between operations: 14.3 us -> 0.67 us
    all_gather x2 -> x0, waiting for transfers between devices: 990 us -> none  [the longest x1 842 us: shards(): operator_blocks = lax.all_gather(string_blocks, 'col', axis=0, tiled=True)]
    pallas_call x0 -> x1, Pallas kernels: none -> 124 us  [shards(): pl.pallas_call(kernel, out_shape=jax.ShapeDtypeStruct((24, 3072), F32), i...]
    dot_general x5 -> x0, matrix products: 39.5 us -> none  [the longest x4 35.6 us: apply_blocks(): jnp.einsum('rifk,ifjk->rij', picked, tiles, precision=lax.Precision.HIGHEST)]
    all_to_all x3 -> x0, starting transfers between devices: 35.9 us -> none  [swap_layout(): lax.all_to_all(layout_pieces(stacked), 'col', split_axis=1, concat_axis=1...]
    all_to_all x3 -> x0, waiting for transfers between devices: 30.6 us -> none  [swap_layout(): lax.all_to_all(layout_pieces(stacked), 'col', split_axis=1, concat_axis=1...]
    all_to_all x1 -> x0, blocking collectives: 27.6 us -> none  [swap_layout(): lax.all_to_all(layout_pieces(stacked), 'col', split_axis=1, concat_axis=1...]
  transfers between devices with their start and end apart: 5 -> 0, of which waited for: 5 -> 0; matrix products, arithmetic and copies ran while one was open for 2% -> 0% of each run, Pallas kernels for 0% -> 0%
where the time goes in v2:
time: 129 us
  Pallas kernels  124 us (96%)
  local copies, waits for them, and re-layouts  4.25 us (3%)
    pallas_call x1, Pallas kernels, shards(): pl.pallas_call(kernel, out_shape=jax.ShapeDtypeStruct((24, 3072), F32), i...  124 us
    unnamed x10, local copies, waits for them, and re-layouts  4.25 us

profile of v2, /device:TPU:1, one launch (start us, length us, event | category | flops | bytes accessed | tf_op | source)
XLA Modules:
  0.0 129.0 jit_solution(11797512537385452772)
XLA Ops:
  0.7 0.0 copy-start.3
  0.7 0.8 copy.7.cols_ref
  1.4 0.0 copy-done.3
  1.4 0.0 copy-start
  1.4 1.0 copy-done
  2.4 0.0 copy-start.1
  2.4 1.0 copy-done.1
  3.4 0.0 copy-start.2
  3.4 0.8 copy-done.2
  4.2 124.0 %filter.1 = f32[24,3072]{1,0:T(8,128)S(1)} custom-call(f32[24,3072]{1,0:T(8,128)S(1)} %bitcast.3, f32[24,3072]{1,0:T(8,128)S(1)} %copy-done.1, f32[1]{0:T(128)S(6)} %copy.9.shift_ref, f32[4,4]{1,0:T(4,128)S(1)} %copy-done.3, bf16[240,128]{1,0:T(8,128)(2,1)S(1)} %copy-done.2, s32[24,10]{1,0:T(8,128)S(1)} %copy.7.cols_ref), custom_call_target="tpu_custom_call" | custom-call | tf_op jit(solution)/shard_map/filter/pallas_call | solution.py:474
  128.2 0.7 copy.10
Async XLA Ops:
  0.7 0.8 copy-start.3
  1.4 1.0 copy-start
  2.4 1.0 copy-start.1
  3.4 0.8 copy-start.2

commit v3 on v2

--- a/solution.py
+++ b/solution.py
@@ -85,10 +85,10 @@
     return jnp.concatenate([high, value - high], axis=0).astype(BF16)
 
 
-def kernel(v_ref, diag_ref, shift_ref, rot_ref, mine_ref, cols_ref, out_ref,
-           op, grid_v, grid_t, turn, zs_v, zs_t, zs_f, zs_g, zb_v, zb_t, zb_f, zb_g,
+def kernel(v_any, diag_any, shift_ref, rot_ref, mine_ref, cols_ref, out_ref,
+           v_ref, diag_ref, op, grid_v, grid_t, turn, zs_v, zs_t, zs_f, zs_g, zb_v, zb_t, zb_f, zb_g,
            xb, vc, rv, tb, fm, fsib, pm, psib, fr, pr, wf, wg, ib_f, ib_g, hf, eb,
-           op_send, op_recv, op_local, plane_send, plane_recv, z_send, z_recv, pair_send, pair_recv):
+           op_send, op_recv, local, plane_send, plane_recv, z_send, z_recv, pair_send, pair_recv):
     zh, core, zl = lax.axis_index("zh"), lax.axis_index("core"), lax.axis_index("zl")
     y, x = lax.axis_index("y"), lax.axis_index("x")
     z = zh * 8 + zl
@@ -102,9 +102,6 @@
 
     pair = {"zh": zh, "core": 1 - core, "zl": zl, "y": y, "x": x}
 
-    energy = shift_ref[0]
-    eb[zh] = jnp.full((8, 128), energy, F32)
-    turn[...] = jnp.zeros_like(turn)
     barrier = pltpu.get_barrier_semaphore()
 
     @pl.loop(1, 16)
@@ -113,6 +110,37 @@
         pl.semaphore_signal(barrier, inc=1, device_id=at_p(lax.rem(p + step, 16)), device_id_type=ONTO)
 
     pl.semaphore_signal(barrier, inc=1, device_id=pair, device_id_type=ONTO)
+    load_v = pltpu.make_async_copy(v_any.at[0], v_ref, local.at[0])
+    load_diag = pltpu.make_async_copy(diag_any, diag_ref, local.at[1])
+    load_v.start()
+    load_diag.start()
+
+    @pl.when(core == 0)
+    def _():
+        part = pl.ds(0, CUT)
+        load = pltpu.make_async_copy(mine_ref.at[part], op.at[zl, y, x, part], local.at[2])
+        load.start()
+        load.wait()
+
+    @pl.when(core == 1)
+    def _():
+        part = pl.ds(CUT, 240 - CUT)
+        load = pltpu.make_async_copy(mine_ref.at[part], op.at[zl, y, x, part], local.at[2])
+        load.start()
+        load.wait()
+
+    energy = shift_ref[0]
+    eb[zh] = jnp.full((8, 128), energy, F32)
+    turn[...] = jnp.zeros_like(turn)
+    load_v.wait()
+    load_diag.wait()
+    grid_v[pl.ds(pl.multiple_of(p * 24, 8), 24), :] = v_ref[
+        :, pl.ds(pl.multiple_of((3 * (p // 2) + lax.rem(p, 2)) * 128, 128), 256)]
+
+    @pl.loop(0, 24)
+    def _(c):
+        xb[c] = split(v_ref[:, pl.ds(pl.multiple_of(c * 128, 128), 128)])
+
     pl.semaphore_wait(barrier, 31)
 
     def plane_copy(kind, src, dst, to, source):
@@ -192,10 +220,6 @@
                 body(*spread(color))
 
     def spread_start(rows, copy):
-        part = pl.ds(rows[0], rows[1])
-        own = pltpu.make_async_copy(mine_ref.at[part], op.at[zl, y, x, part], op_local)
-        own.start()
-        own.wait()
         for number in range(7):
             copy(number).start()
 
@@ -283,7 +307,7 @@
         def _(step):
             m = lax.rem(first + step, 8)
             for ii in range(3):
-                vectors = jnp.concatenate([xb[cols_ref[3 * m + ii, f]] for f in range(10)], axis=1)
+                vectors = jnp.concatenate([xb[cols_ref[f, 3 * m + ii]] for f in range(10)], axis=1)
                 blocks = jnp.concatenate([block(m, ii, f) for f in range(10)], axis=1)
                 both = lax.dot_general(vectors, blocks, (((1,), (1,)), ((), ())), preferred_element_type=F32)
                 emit(m, ii, both[0:24] + both[24:48])
@@ -293,22 +317,17 @@
     def lanes(m, ii):
         return pl.ds(pl.multiple_of((3 * m + ii) * 128, 128), 128)
 
+    by_color(spread_start)
+
     @pl.loop(1, 16)
     def _(step):
         target = lax.rem(p + step, 16)
         plane_copy(0, v_ref.at[:, window(target)], grid_v.at[mine24, :], target, p).start()
 
-    grid_v[mine24, :] = v_ref[:, window(p)]
-    by_color(spread_start)
     energy_copy = pltpu.make_async_remote_copy(
         src_ref=eb.at[zh], dst_ref=eb.at[zh], send_sem=pair_send.at[2], recv_sem=pair_recv.at[2],
         device_id=at_z(lax.rem(z + 8, 16)), device_id_type=ONTO)
     energy_copy.start()
-
-    @pl.loop(0, 8)
-    def _(m):
-        for ii in range(3):
-            xb[3 * m + ii] = split(v_ref[:, lanes(m, ii)])
 
     by_color(spread_on)
     wait_plane(0, lambda other: rows24(grid_v, other))
@@ -465,6 +484,8 @@
 def shards(coeffs, diagonal, shift, rotation, string_blocks, block_cols):
     vmem = pl.BlockSpec(memory_space=pltpu.VMEM)
     smem = pl.BlockSpec(memory_space=pltpu.SMEM)
+    hbm = pl.BlockSpec(memory_space=pltpu.HBM)
+    rows = pltpu.VMEM((24, 3072), F32)
     grid = pltpu.VMEM((384, 256), F32)
     packed = pltpu.VMEM((16, 36, 128), F32)
     chunks = pltpu.VMEM((24, 24, 128), F32)
@@ -474,10 +495,10 @@
     result = pl.pallas_call(
         kernel,
         out_shape=jax.ShapeDtypeStruct((24, 3072), F32),
-        in_specs=[vmem, vmem, smem, smem, vmem, smem],
+        in_specs=[hbm, hbm, smem, smem, hbm, smem],
         out_specs=vmem,
         scratch_shapes=[
-            pltpu.VMEM((8, 4, 4, 240, 128), BF16),
+            rows, rows, pltpu.VMEM((8, 4, 4, 240, 128), BF16),
             grid, grid, pltpu.VMEM((256, 128), F32),
             packed, packed, packed, packed, packed, packed, packed, packed,
             pltpu.VMEM((24, 48, 128), BF16),
@@ -485,13 +506,13 @@
             chunks, chunks, chunks, chunks, chunks, chunks,
             grid, grid, windows, windows, wide,
             pltpu.VMEM((2, 8, 128), F32),
-            dma((len(PLAN),)), dma((len(PLAN),)), dma,
+            dma((len(PLAN),)), dma((len(PLAN),)), dma((3,)),
             dma((4, 16)), dma((4, 16)), dma((4, 16)), dma((4, 16)), dma((3,)), dma((3,)),
         ],
         compiler_params=pltpu.CompilerParams(
             collective_id=0, has_side_effects=True, vmem_limit_bytes=48 * 1024 * 1024),
         name="filter",
-    )(coeffs[0], diagonal, shift, rotation, string_blocks, block_cols)
+    )(coeffs, diagonal, shift, rotation, string_blocks, block_cols.T)
     return result[None]
 
 

time: 129 us -> 130 us (level)
    unnamed x10 -> x11, local copies, waits for them, and re-layouts: 4.25 us -> 4.18 us
where the time goes in v3:
time: 130 us
  Pallas kernels  125 us (96%)
  local copies, waits for them, and re-layouts  4.18 us (3%)
    pallas_call x1, Pallas kernels, shards(): pl.pallas_call(kernel, out_shape=jax.ShapeDtypeStruct((24, 3072), F32), i...  125 us
    unnamed x11, local copies, waits for them, and re-layouts  4.18 us

profile of v3, /device:TPU:1, one launch (start us, length us, event | category | flops | bytes accessed | tf_op | source)
XLA Modules:
  0.0 129.6 jit_solution(17353725671703806596)
XLA Ops:
  0.0 0.0 copy-start.4
  0.7 0.0 copy-done.4
  0.7 0.0 copy-start
  0.7 1.0 copy-done
  1.6 0.0 copy-start.1
  1.6 1.0 copy-done.1
  2.6 0.0 copy-start.2
  2.6 0.8 copy-done.2
  3.4 0.0 copy-start.3
  3.4 0.7 copy-done.3
  4.1 124.8 %filter.1 = f32[24,3072]{1,0:T(8,128)S(1)} custom-call(f32[1,24,3072]{2,1,0:T(8,128)S(1)} %copy-done, f32[24,3072]{1,0:T(8,128)S(1)} %copy-done.1, f32[1]{0:T(128)S(6)} %copy.8.shift_ref, f32[4,4]{1,0:T(4,128)S(1)} %copy-done.4, bf16[240,128]{1,0:T(8,128)(2,1)S(1)} %copy-done.2, s32[10,24]{1,0:T(8,128)S(1)} %bitcast.3), custom_call_target="tpu_custom_call" | custom-call | tf_op jit(solution)/shard_map/filter/pallas_call | solution.py:495
  128.9 0.7 copy.9
Async XLA Ops:
  0.0 0.7 copy-start.4
  0.7 1.0 copy-start
  1.6 1.0 copy-start.1
  2.6 0.8 copy-start.2
  3.4 0.7 copy-start.3

commit v4 on v3

--- a/solution.py
+++ b/solution.py
@@ -9,6 +9,7 @@
 ROOT = ("zh", "core")
 COL = ("zl", "y", "x")
 CUT = 128
+PARTS = (((0, 96), (96, 32)), ((CUT, 80), (CUT + 80, 32)))
 F32, BF16 = jnp.float32, jnp.bfloat16
 ONTO = pl.DeviceIdType.MESH
 
@@ -66,14 +67,44 @@
         sibling(zs, a, 1)
         steps.append((number + 1, (n, len(plan))))
         last.append((n, high, a))
+    lasts = []
     for number, zs, a in last:
         n = len(plan)
         sibling(zs, a, 2)
-        steps.append((number, (n, len(plan))))
-    return plan, marks, steps
-
-
-PLAN, MARKS, STEPS = spread_plan()
+        lasts.append((number, (n, len(plan))))
+
+    def ring(part, half, way):
+        plan.append((("ring", part, half), ("z", way), ("ring", part - way, half)))
+        return len(plan) - 1
+
+    def ring_sibling(part, half=None):
+        plan.append((("ring", part, half), ("core", 1), "sibling"))
+
+    n = len(plan)
+    up, down = ring(0, None, 1), ring(0, None, -1)
+    ring_sibling(0)
+    marks["ring"] = (n, len(plan))
+    rings = []
+    for hop in (1, 2, 3):
+        n = len(plan)
+        next_up = ring(-hop, 0 if hop == 3 else None, 1)
+        ring_sibling(-hop)
+        rings.append((up, (n, len(plan))))
+        n = len(plan)
+        next_down = ring(hop, 1 if hop == 3 else None, -1)
+        ring_sibling(hop)
+        rings.append((down, (n, len(plan))))
+        up, down = next_up, next_down
+    for number, part, half in ((up, -4, 0), (down, 4, 1)):
+        n = len(plan)
+        ring_sibling(part, half)
+        rings.append((number, (n, len(plan))))
+    early = steps[0:2] + rings[0:2] + steps[2:8] + rings[2:4] + steps[8:12] + rings[4:6]
+    late = steps[12:] + lasts + rings[6:8]
+    return plan, marks, early, late
+
+
+PLAN, MARKS, EARLY, LATE = spread_plan()
 
 
 def device(z, y, x, core):
@@ -87,6 +118,7 @@
 
 def kernel(v_any, diag_any, shift_ref, rot_ref, mine_ref, cols_ref, out_ref,
            v_ref, diag_ref, op, grid_v, grid_t, turn, zs_v, zs_t, zs_f, zs_g, zb_v, zb_t, zb_f, zb_g,
+           sent_v, sent_t, sent_f, sent_g, got_v, got_t, got_f, got_g,
            xb, vc, rv, tb, fm, fsib, pm, psib, fr, pr, wf, wg, ib_f, ib_g, hf, eb,
            op_send, op_recv, local, plane_send, plane_recv, z_send, z_recv, pair_send, pair_recv):
     zh, core, zl = lax.axis_index("zh"), lax.axis_index("core"), lax.axis_index("zl")
@@ -181,12 +213,15 @@
             z_copy(kind, ref.at[other], ref.at[other], other, other).wait_send()
 
     def spread(color):
-        rows = (0, CUT) if color == 0 else (CUT, 240 - CUT)
-        others = (CUT, 240 - CUT) if color == 0 else (0, CUT)
+        rows, around = PARTS[color]
+        others, others_around = PARTS[1 - color]
         place = {"y": y, "x": x}
 
         def of(piece, part, first, second):
             zs, a, b = piece
+            if zs == "ring":
+                which = pl.ds(0, 4) if b is None else pl.ds(2 * b, 2)
+                return op.at[lax.rem(zl + a + 8, 8), which, :, pl.ds(part[0], part[1])]
             index = {first: lax.rem(place[first] + a + 4, 4), second: lax.rem(place[second] + b + 4, 4)}
             return op.at[pl.ds(zs[0], zs[1]), index["y"], index["x"], pl.ds(part[0], part[1])]
 
@@ -199,8 +234,13 @@
                 ref = op.at[source, y, x, pl.ds(rows[0], rows[1])]
                 to = at_z(lax.rem(z + step + 16, 16))
             elif axis == "core":
-                ref = of(piece, others, second, first) if landing else of(piece, rows, first, second)
+                going = around if piece[0] == "ring" else rows
+                coming = others_around if piece[0] == "ring" else others
+                ref = of(piece, coming, second, first) if landing else of(piece, going, first, second)
                 to = pair
+            elif axis == "z":
+                ref = of(lands if landing else piece, around, first, second)
+                to = at_z(lax.rem(z + step + 16, 16))
             else:
                 ref = of(lands if landing else piece, rows, first, second)
                 name = first if axis == "first" else second
@@ -211,7 +251,7 @@
                 src_ref=ref, dst_ref=ref, send_sem=op_send.at[number], recv_sem=op_recv.at[number],
                 device_id=to, device_id_type=ONTO)
 
-        return rows, copy
+        return around, copy
 
     def by_color(body):
         for color in (0, 1):
@@ -219,28 +259,54 @@
             def _():
                 body(*spread(color))
 
-    def spread_start(rows, copy):
+    def spread_start(around, copy):
         for number in range(7):
             copy(number).start()
 
-    def spread_on(rows, copy):
+        @pl.loop(1, 16)
+        def _(step):
+            target = lax.rem(p + step, 16)
+            around_copy(around, p, target, p).start()
+
+    def around_copy(around, source_slot, to, source):
+        ref = op.at[zl, source_slot // 4, lax.rem(source_slot, 4), pl.ds(around[0], around[1])]
+        return plane_copy(4, ref, ref, to, source)
+
+    def spread_on(around, copy):
         for number in range(7):
             copy(number, True).wait_recv()
         for number in range(*MARKS["start"]):
             copy(number).start()
 
-    def spread_rest(rows, copy):
-        for number, (low, high) in STEPS:
+        @pl.loop(1, 16)
+        def _(step):
+            other = lax.rem(p + step, 16)
+            around_copy(around, other, other, other).wait_recv()
+
+        for number in range(*MARKS["ring"]):
+            copy(number).start()
+        follow_on(EARLY[:4], copy)
+
+    def follow_on(steps, copy):
+        for number, (low, high) in steps:
             copy(number, True).wait_recv()
             for follow in range(low, high):
                 copy(follow).start()
+
+    def spread_rest(around, copy):
+        follow_on(EARLY[4:] + LATE, copy)
         for number in range(len(PLAN)):
             if PLAN[number][1][0] == "core":
                 copy(number, True).wait_recv()
 
-    def spread_sent(rows, copy):
+    def spread_sent(around, copy):
         for number in range(len(PLAN)):
             copy(number).wait_send()
+
+        @pl.loop(1, 16)
+        def _(step):
+            other = lax.rem(p + step, 16)
+            around_copy(around, p, other, other).wait_send()
 
     def window(target):
         return pl.ds(pl.multiple_of((3 * (target // 2) + lax.rem(target, 2)) * 128, 128), 256)
@@ -257,6 +323,27 @@
             for target in range(16):
                 zs[target, 12 * k:12 * k + 12, :] = columns[12 * target:12 * target + 12]
 
+    own_lane = lax.broadcasted_iota(jnp.int32, (36, 128), 0) == lax.broadcasted_iota(jnp.int32, (36, 128), 1)
+
+    def encode(zs, codes, target):
+        value = zs[target]
+        top = jnp.maximum(jnp.max(jnp.abs(value), axis=1, keepdims=True), 1e-30)
+        level = jnp.ceil(jnp.log2(top) * 128.0)
+        scaled = jnp.round(value * (jnp.exp2(level * (-1.0 / 128.0)) * 32700.0))
+        levels = jnp.sum(jnp.where(own_lane, level, 0.0), axis=0, keepdims=True)
+        whole = jnp.concatenate([scaled, jnp.broadcast_to(levels, (4, 128))], axis=0)
+        codes[target] = whole.astype(jnp.int32).astype(jnp.int16)
+
+    def decode(codes, zb):
+        @pl.loop(0, 4)
+        def _(quarter):
+            for one in range(4):
+                source = quarter * 4 + one
+                whole = codes[source].astype(jnp.int32).astype(F32)
+                levels = jnp.broadcast_to(whole[36:37], (36, 128))
+                level = jnp.sum(jnp.where(own_lane, levels, 0.0), axis=1, keepdims=True)
+                zb[source] = whole[0:36] * (jnp.exp2(level * (1.0 / 128.0)) * (1.0 / 32700.0))
+
     def send_z(kind, zs, zb, target):
         @pl.when(target != z)
         def _():
@@ -266,10 +353,14 @@
         def _():
             zb[z] = zs[z]
 
-    def send_all_z(kind, zs, zb):
-        @pl.loop(0, 16)
-        def _(step):
-            send_z(kind, zs, zb, lax.rem(z + 8 + step, 16))
+    def send_all_z(kind, zs, codes, landing):
+        @pl.loop(0, 4)
+        def _(step):
+            group = [lax.rem(z + 8 + 4 * step + one, 16) for one in range(4)]
+            for target in group:
+                encode(zs, codes, target)
+            for target in group:
+                send_z(kind, codes, landing, target)
 
     def turn_columns(zb, rows_out):
         for k in range(3):
@@ -332,7 +423,7 @@
     by_color(spread_on)
     wait_plane(0, lambda other: rows24(grid_v, other))
     turn_rows(grid_v, zs_v)
-    send_all_z(0, zs_v, zb_v)
+    send_all_z(0, zs_v, sent_v, got_v)
     by_color(spread_rest)
 
     def emit_t(m, ii, value):
@@ -356,9 +447,10 @@
 
     wait_plane(1, lambda other: rows24(grid_t, other))
     turn_rows(grid_t, zs_t)
-    send_all_z(1, zs_t, zb_t)
-
-    wait_z(0, zb_v)
+    send_all_z(1, zs_t, sent_t, got_t)
+
+    wait_z(0, got_v)
+    decode(got_v, zb_v)
 
     @pl.loop(0, 8)
     def _(m):
@@ -372,7 +464,8 @@
         rv[3 * m + ii] = value
 
     operate(0, emit_rv)
-    wait_z(1, zb_t)
+    wait_z(1, got_t)
+    decode(got_t, zb_t)
 
     other_energy = pltpu.make_async_remote_copy(
         src_ref=eb.at[1 - zh], dst_ref=eb.at[1 - zh], send_sem=pair_send.at[2], recv_sem=pair_recv.at[2],
@@ -425,8 +518,10 @@
             xb[c] = split(value)
             zs_f[m, 12 * k:12 * k + 12, :] = value[0:12]
             zs_f[8 + m, 12 * k:12 * k + 12, :] = value[12:24]
-        send_z(2, zs_f, zb_f, m)
-        send_z(2, zs_f, zb_f, m + 8)
+        encode(zs_f, sent_f, m)
+        encode(zs_f, sent_f, m + 8)
+        send_z(2, sent_f, got_f, m)
+        send_z(2, sent_f, got_f, m + 8)
 
     pair_copy(1, psib, pr).wait_recv()
 
@@ -437,14 +532,21 @@
         zs_g[8 + m, 12 * ii:12 * ii + 12, :] = g[12:24]
 
     def after_g(m):
-        send_z(3, zs_g, zb_g, m)
-        send_z(3, zs_g, zb_g, m + 8)
+        encode(zs_g, sent_g, m)
+        encode(zs_g, sent_g, m + 8)
+        send_z(3, sent_g, got_g, m)
+        send_z(3, sent_g, got_g, m + 8)
 
     operate(zl, emit_g, after_g)
 
-    wait_z(2, zb_f)
+    wait_z(2, got_f)
+    decode(got_f, zb_f)
     turn_columns(zb_f, wf)
     send_rows(2, wf, ib_f)
+    wait_z(3, got_g)
+    decode(got_g, zb_g)
+    turn_columns(zb_g, wg)
+    send_rows(3, wg, ib_g)
     wait_plane(2, lambda other: ib_f.at[other])
 
     @pl.loop(0, 8)
@@ -458,9 +560,6 @@
         out_ref[:, here] = value + diag_ref[:, here] * hf[m, :, 128 * ii:128 * ii + 128]
 
     operate(0, emit_out)
-    wait_z(3, zb_g)
-    turn_columns(zb_g, wg)
-    send_rows(3, wg, ib_g)
     wait_plane(3, lambda other: ib_g.at[other])
 
     @pl.loop(0, 8)
@@ -477,7 +576,7 @@
     sent_plane(1, lambda other: rows24(grid_t, other))
     sent_plane(2, lambda other: ib_f.at[other])
     sent_plane(3, lambda other: ib_g.at[other])
-    for kind, ref in enumerate((zs_v, zs_t, zs_f, zs_g)):
+    for kind, ref in enumerate((sent_v, sent_t, sent_f, sent_g)):
         sent_z(kind, ref)
 
 
@@ -488,6 +587,7 @@
     rows = pltpu.VMEM((24, 3072), F32)
     grid = pltpu.VMEM((384, 256), F32)
     packed = pltpu.VMEM((16, 36, 128), F32)
+    coded = pltpu.VMEM((16, 40, 128), jnp.int16)
     chunks = pltpu.VMEM((24, 24, 128), F32)
     windows = pltpu.VMEM((16, 24, 256), F32)
     wide = pltpu.VMEM((8, 24, 384), F32)
@@ -501,16 +601,17 @@
             rows, rows, pltpu.VMEM((8, 4, 4, 240, 128), BF16),
             grid, grid, pltpu.VMEM((256, 128), F32),
             packed, packed, packed, packed, packed, packed, packed, packed,
+            coded, coded, coded, coded, coded, coded, coded, coded,
             pltpu.VMEM((24, 48, 128), BF16),
             chunks, chunks, wide,
             chunks, chunks, chunks, chunks, chunks, chunks,
             grid, grid, windows, windows, wide,
             pltpu.VMEM((2, 8, 128), F32),
             dma((len(PLAN),)), dma((len(PLAN),)), dma((3,)),
-            dma((4, 16)), dma((4, 16)), dma((4, 16)), dma((4, 16)), dma((3,)), dma((3,)),
+            dma((5, 16)), dma((5, 16)), dma((4, 16)), dma((4, 16)), dma((3,)), dma((3,)),
         ],
         compiler_params=pltpu.CompilerParams(
-            collective_id=0, has_side_effects=True, vmem_limit_bytes=48 * 1024 * 1024),
+            collective_id=0, has_side_effects=True, vmem_limit_bytes=67043328),
         name="filter",
     )(coeffs, diagonal, shift, rotation, string_blocks, block_cols.T)
     return result[None]

time: 130 us -> 107 us (0.82)
  Pallas kernels: 125 us -> 104 us
  local copies, waits for them, and re-layouts: 4.18 us -> 1.69 us
    pallas_call x1, Pallas kernels: 125 us -> 104 us  [shards(): pl.pallas_call(kernel, out_shape=jax.ShapeDtypeStruct((24, 3072), F32), i...]
    unnamed x11 -> x1, local copies, waits for them, and re-layouts: 4.18 us -> 1.69 us
where the time goes in v4:
time: 107 us
  Pallas kernels  104 us (97%)
  local copies, waits for them, and re-layouts  1.69 us (2%)
    pallas_call x1, Pallas kernels, shards(): pl.pallas_call(kernel, out_shape=jax.ShapeDtypeStruct((24, 3072), F32), i...  104 us

profile of v4, /device:TPU:1, one launch (start us, length us, event | category | flops | bytes accessed | tf_op | source)
XLA Modules:
  0.0 106.5 jit_solution(11715641910328253278)
XLA Ops:
  0.7 104.2 %filter.1 = f32[24,3072]{1,0:T(8,128)} custom-call(f32[1,24,3072]{2,1,0:T(8,128)} %v_any.1, f32[24,3072]{1,0:T(8,128)} %diag_any.1, f32[1]{0:T(128)S(6)} %copy.8.shift_ref, f32[4,4]{1,0:T(4,128)} %rot_ref.1, bf16[240,128]{1,0:T(8,128)(2,1)} %mine_ref.1, s32[10,24]{1,0:T(8,128)} %bitcast.3), custom_call_target="tpu_custom_call" | custom-call | tf_op jit(solution)/shard_map/filter/pallas_call | solution.py:595
  104.8 1.7 %copy.9 = f32[1,24,3072]{2,1,0:T(8,128)} copy(f32[1,24,3072]{2,1,0:T(8,128)} %bitcast.2) | data formatting | bytes 589824

commit v5 on v4

--- a/solution.py
+++ b/solution.py
@@ -120,7 +120,7 @@
            v_ref, diag_ref, op, grid_v, grid_t, turn, zs_v, zs_t, zs_f, zs_g, zb_v, zb_t, zb_f, zb_g,
            sent_v, sent_t, sent_f, sent_g, got_v, got_t, got_f, got_g,
            xb, vc, rv, tb, fm, fsib, pm, psib, fr, pr, wf, wg, ib_f, ib_g, hf, eb,
-           op_send, op_recv, local, plane_send, plane_recv, z_send, z_recv, pair_send, pair_recv):
+           op_send, op_recv, local, plane_send, plane_recv, z_send, z_recv, pair_send, pair_recv, vouch):
     zh, core, zl = lax.axis_index("zh"), lax.axis_index("core"), lax.axis_index("zl")
     y, x = lax.axis_index("y"), lax.axis_index("x")
     z = zh * 8 + zl
@@ -138,8 +138,10 @@
 
     @pl.loop(1, 16)
     def _(step):
-        pl.semaphore_signal(barrier, inc=1, device_id=at_z(lax.rem(z + step, 16)), device_id_type=ONTO)
         pl.semaphore_signal(barrier, inc=1, device_id=at_p(lax.rem(p + step, 16)), device_id_type=ONTO)
+
+    for step in (4, -4, 3, -3, 2, -2, 1, -1):
+        pl.semaphore_signal(barrier, inc=1, device_id=at_z(lax.rem(z + step + 16, 16)), device_id_type=ONTO)
 
     pl.semaphore_signal(barrier, inc=1, device_id=pair, device_id_type=ONTO)
     load_v = pltpu.make_async_copy(v_any.at[0], v_ref, local.at[0])
@@ -173,7 +175,9 @@
     def _(c):
         xb[c] = split(v_ref[:, pl.ds(pl.multiple_of(c * 128, 128), 128)])
 
-    pl.semaphore_wait(barrier, 31)
+    pl.semaphore_wait(barrier, 24)
+    for step in (4, -4):
+        pl.semaphore_signal(vouch, inc=1, device_id=at_z(lax.rem(z + step + 16, 16)), device_id_type=ONTO)
 
     def plane_copy(kind, src, dst, to, source):
         return pltpu.make_async_remote_copy(
@@ -356,7 +360,8 @@
     def send_all_z(kind, zs, codes, landing):
         @pl.loop(0, 4)
         def _(step):
-            group = [lax.rem(z + 8 + 4 * step + one, 16) for one in range(4)]
+            group = [lax.rem(z + 16 + way, 16) for way in
+                     (2 * step - 8, 7 - 2 * step, 2 * step - 7, 6 - 2 * step)]
             for target in group:
                 encode(zs, codes, target)
             for target in group:
@@ -393,10 +398,13 @@
             row, left = row + take, left - take
         return parts[0] if len(parts) == 1 else jnp.concatenate(parts, axis=0)
 
-    def operate(first, emit, after=None):
+    def outward(step):
+        return jnp.where(lax.rem(step, 2) == 1, (step + 1) // 2, 8 - step // 2)
+
+    def operate(first, emit, after=None, order=lambda step: step):
         @pl.loop(0, 8)
         def _(step):
-            m = lax.rem(first + step, 8)
+            m = lax.rem(first + order(step), 8)
             for ii in range(3):
                 vectors = jnp.concatenate([xb[cols_ref[f, 3 * m + ii]] for f in range(10)], axis=1)
                 blocks = jnp.concatenate([block(m, ii, f) for f in range(10)], axis=1)
@@ -415,12 +423,13 @@
         target = lax.rem(p + step, 16)
         plane_copy(0, v_ref.at[:, window(target)], grid_v.at[mine24, :], target, p).start()
 
+
+    by_color(spread_on)
+    pl.semaphore_wait(vouch, 2)
     energy_copy = pltpu.make_async_remote_copy(
         src_ref=eb.at[zh], dst_ref=eb.at[zh], send_sem=pair_send.at[2], recv_sem=pair_recv.at[2],
         device_id=at_z(lax.rem(z + 8, 16)), device_id_type=ONTO)
     energy_copy.start()
-
-    by_color(spread_on)
     wait_plane(0, lambda other: rows24(grid_v, other))
     turn_rows(grid_v, zs_v)
     send_all_z(0, zs_v, sent_v, got_v)
@@ -484,6 +493,11 @@
 
     def swapped(value):
         return jnp.concatenate([value[12:24], value[0:12]], axis=0)
+
+    def pair_copy(index, src, dst):
+        return pltpu.make_async_remote_copy(
+            src_ref=src, dst_ref=dst, send_sem=pair_send.at[index], recv_sem=pair_recv.at[index],
+            device_id=pair, device_id_type=ONTO)
 
     @pl.loop(0, 8)
     def _(m):
@@ -493,25 +507,27 @@
             t = jnp.concatenate([zb_t[m, part, :], zb_t[8 + m, part, :]], axis=0)
             first = 0.5 * (rv[c] + t)
             turned = swapped(first)
-            rest = shifts * first + vc[c]
-            rest_turned = swapped(rest)
+            rv[c] = first
             fm[c] = here_straight * first + here_crossed * turned
             fsib[c] = there_straight * first + there_crossed * turned
+
+    pair_copy(0, fsib, fr).start()
+
+    @pl.loop(0, 8)
+    def _(m):
+        for k in range(3):
+            c = 3 * m + k
+            rest = shifts * rv[c] + vc[c]
+            rest_turned = swapped(rest)
             pm[c] = here_straight * rest + here_crossed * rest_turned
             psib[c] = there_straight * rest + there_crossed * rest_turned
 
-    def pair_copy(index, src, dst):
-        return pltpu.make_async_remote_copy(
-            src_ref=src, dst_ref=dst, send_sem=pair_send.at[index], recv_sem=pair_recv.at[index],
-            device_id=pair, device_id_type=ONTO)
-
-    pair_copy(0, fsib, fr).start()
     pair_copy(1, psib, pr).start()
     pair_copy(0, fsib, fr).wait_recv()
 
     @pl.loop(0, 8)
     def _(step):
-        m = lax.rem(zl + step, 8)
+        m = lax.rem(zl + outward(step), 8)
         for k in range(3):
             c = 3 * m + k
             value = fm[c] + fr[c]
@@ -537,7 +553,7 @@
         send_z(3, sent_g, got_g, m)
         send_z(3, sent_g, got_g, m + 8)
 
-    operate(zl, emit_g, after_g)
+    operate(zl, emit_g, after_g, outward)
 
     wait_z(2, got_f)
     decode(got_f, zb_f)
@@ -609,6 +625,7 @@
             pltpu.VMEM((2, 8, 128), F32),
             dma((len(PLAN),)), dma((len(PLAN),)), dma((3,)),
             dma((5, 16)), dma((5, 16)), dma((4, 16)), dma((4, 16)), dma((3,)), dma((3,)),
+            pltpu.SemaphoreType.REGULAR,
         ],
         compiler_params=pltpu.CompilerParams(
             collective_id=0, has_side_effects=True, vmem_limit_bytes=67043328),

time: 107 us -> 102 us (0.953)
  Pallas kernels: 104 us -> 99.7 us
    pallas_call x1, Pallas kernels: 104 us -> 99.7 us  [shards(): pl.pallas_call(kernel, out_shape=jax.ShapeDtypeStruct((24, 3072), F32), i...]
where the time goes in v5:
time: 102 us
  Pallas kernels  99.7 us (98%)
  local copies, waits for them, and re-layouts  1.69 us (2%)
    pallas_call x1, Pallas kernels, shards(): pl.pallas_call(kernel, out_shape=jax.ShapeDtypeStruct((24, 3072), F32), i...  99.7 us

profile of v5, /device:TPU:1, one launch (start us, length us, event | category | flops | bytes accessed | tf_op | source)
XLA Modules:
  0.0 102.0 jit_solution(11313354461336293763)
XLA Ops:
  0.7 99.7 %filter.1 = f32[24,3072]{1,0:T(8,128)} custom-call(f32[1,24,3072]{2,1,0:T(8,128)} %v_any.1, f32[24,3072]{1,0:T(8,128)} %diag_any.1, f32[1]{0:T(128)S(6)} %copy.8.shift_ref, f32[4,4]{1,0:T(4,128)} %rot_ref.1, bf16[240,128]{1,0:T(8,128)(2,1)} %mine_ref.1, s32[10,24]{1,0:T(8,128)} %bitcast.3), custom_call_target="tpu_custom_call" | custom-call | tf_op jit(solution)/shard_map/filter/pallas_call | solution.py:611
  100.3 1.7 %copy.9 = f32[1,24,3072]{2,1,0:T(8,128)} copy(f32[1,24,3072]{2,1,0:T(8,128)} %bitcast.2) | data formatting | bytes 589824

commit v6 on v5

--- a/solution.py
+++ b/solution.py
@@ -146,14 +146,13 @@
     pl.semaphore_signal(barrier, inc=1, device_id=pair, device_id_type=ONTO)
     load_v = pltpu.make_async_copy(v_any.at[0], v_ref, local.at[0])
     load_diag = pltpu.make_async_copy(diag_any, diag_ref, local.at[1])
-    load_v.start()
-    load_diag.start()
-
     @pl.when(core == 0)
     def _():
         part = pl.ds(0, CUT)
         load = pltpu.make_async_copy(mine_ref.at[part], op.at[zl, y, x, part], local.at[2])
         load.start()
+        load_v.start()
+        load_diag.start()
         load.wait()
 
     @pl.when(core == 1)
@@ -161,19 +160,9 @@
         part = pl.ds(CUT, 240 - CUT)
         load = pltpu.make_async_copy(mine_ref.at[part], op.at[zl, y, x, part], local.at[2])
         load.start()
+        load_v.start()
+        load_diag.start()
         load.wait()
-
-    energy = shift_ref[0]
-    eb[zh] = jnp.full((8, 128), energy, F32)
-    turn[...] = jnp.zeros_like(turn)
-    load_v.wait()
-    load_diag.wait()
-    grid_v[pl.ds(pl.multiple_of(p * 24, 8), 24), :] = v_ref[
-        :, pl.ds(pl.multiple_of((3 * (p // 2) + lax.rem(p, 2)) * 128, 128), 256)]
-
-    @pl.loop(0, 24)
-    def _(c):
-        xb[c] = split(v_ref[:, pl.ds(pl.multiple_of(c * 128, 128), 128)])
 
     pl.semaphore_wait(barrier, 24)
     for step in (4, -4):
@@ -197,12 +186,6 @@
         def _(step):
             other = lax.rem(p + step, 16)
             plane_copy(kind, slot(other), slot(other), other, other).wait_recv()
-
-    def wait_z(kind, ref):
-        @pl.loop(1, 16)
-        def _(step):
-            other = lax.rem(z + step, 16)
-            z_copy(kind, ref.at[other], ref.at[other], other, other).wait_recv()
 
     def sent_plane(kind, slot):
         @pl.loop(1, 16)
@@ -338,11 +321,19 @@
         whole = jnp.concatenate([scaled, jnp.broadcast_to(levels, (4, 128))], axis=0)
         codes[target] = whole.astype(jnp.int32).astype(jnp.int16)
 
-    def decode(codes, zb):
+    def decode(kind, codes, zb):
         @pl.loop(0, 4)
-        def _(quarter):
-            for one in range(4):
-                source = quarter * 4 + one
+        def _(step):
+            ways = (2 * step - 8, 7 - 2 * step, 2 * step - 7, 6 - 2 * step)
+            for one, way in enumerate(ways):
+                source = lax.rem(z + 16 + way, 16)
+                arriving = z_copy(kind, codes.at[source], codes.at[source], source, source)
+                if one < 3:
+                    arriving.wait_recv()
+                else:
+                    pl.when(step < 3)(arriving.wait_recv)
+            for way in ways:
+                source = lax.rem(z + 16 + way, 16)
                 whole = codes[source].astype(jnp.int32).astype(F32)
                 levels = jnp.broadcast_to(whole[36:37], (36, 128))
                 level = jnp.sum(jnp.where(own_lane, levels, 0.0), axis=1, keepdims=True)
@@ -417,12 +408,24 @@
         return pl.ds(pl.multiple_of((3 * m + ii) * 128, 128), 128)
 
     by_color(spread_start)
+    load_v.wait()
 
     @pl.loop(1, 16)
     def _(step):
         target = lax.rem(p + step, 16)
         plane_copy(0, v_ref.at[:, window(target)], grid_v.at[mine24, :], target, p).start()
 
+
+    energy = shift_ref[0]
+    eb[zh] = jnp.full((8, 128), energy, F32)
+    turn[...] = jnp.zeros_like(turn)
+    load_diag.wait()
+    grid_v[pl.ds(pl.multiple_of(p * 24, 8), 24), :] = v_ref[
+        :, pl.ds(pl.multiple_of((3 * (p // 2) + lax.rem(p, 2)) * 128, 128), 256)]
+
+    @pl.loop(0, 24)
+    def _(c):
+        xb[c] = split(v_ref[:, pl.ds(pl.multiple_of(c * 128, 128), 128)])
 
     by_color(spread_on)
     pl.semaphore_wait(vouch, 2)
@@ -458,8 +461,7 @@
     turn_rows(grid_t, zs_t)
     send_all_z(1, zs_t, sent_t, got_t)
 
-    wait_z(0, got_v)
-    decode(got_v, zb_v)
+    decode(0, got_v, zb_v)
 
     @pl.loop(0, 8)
     def _(m):
@@ -473,8 +475,7 @@
         rv[3 * m + ii] = value
 
     operate(0, emit_rv)
-    wait_z(1, got_t)
-    decode(got_t, zb_t)
+    decode(1, got_t, zb_t)
 
     other_energy = pltpu.make_async_remote_copy(
         src_ref=eb.at[1 - zh], dst_ref=eb.at[1 - zh], send_sem=pair_send.at[2], recv_sem=pair_recv.at[2],
@@ -555,12 +556,10 @@
 
     operate(zl, emit_g, after_g, outward)
 
-    wait_z(2, got_f)
-    decode(got_f, zb_f)
+    decode(2, got_f, zb_f)
     turn_columns(zb_f, wf)
     send_rows(2, wf, ib_f)
-    wait_z(3, got_g)
-    decode(got_g, zb_g)
+    decode(3, got_g, zb_g)
     turn_columns(zb_g, wg)
     send_rows(3, wg, ib_g)
     wait_plane(2, lambda other: ib_f.at[other])
@@ -628,9 +627,10 @@
             pltpu.SemaphoreType.REGULAR,
         ],
         compiler_params=pltpu.CompilerParams(
-            collective_id=0, has_side_effects=True, vmem_limit_bytes=67043328),
+            collective_id=0, has_side_effects=True, vmem_limit_bytes=50331648),
         name="filter",
-    )(coeffs, diagonal, shift, rotation, string_blocks, block_cols.T)
+    )(*(pltpu.with_memory_space_constraint(a, pltpu.HBM) for a in (coeffs, diagonal)), shift, rotation,
+      pltpu.with_memory_space_constraint(string_blocks, pltpu.HBM), block_cols.T)
     return result[None]
 
 

time: 102 us -> 100 us (0.980)
  Pallas kernels: 99.7 us -> 98.1 us
    pallas_call x1, Pallas kernels: 99.7 us -> 98.1 us  [shards(): pl.pallas_call(kernel, out_shape=jax.ShapeDtypeStruct((24, 3072), F32), i...]
where the time goes in v6:
time: 100 us
  Pallas kernels  98.1 us (98%)
  local copies, waits for them, and re-layouts  1.43 us (1%)
    pallas_call x1, Pallas kernels, shards(): pl.pallas_call(kernel, out_shape=jax.ShapeDtypeStruct((24, 3072), F32), i...  98.1 us

profile of v6, /device:TPU:1, one launch (start us, length us, event | category | flops | bytes accessed | tf_op | source)
XLA Modules:
  0.0 100.2 jit_solution(17051440631809760608)
XLA Ops:
  0.0 0.0 copy-start.1
  0.7 0.0 copy-done.1
  0.7 0.0 copy-start
  0.7 0.7 copy-done
  1.4 98.1 %filter.1 = f32[24,3072]{1,0:T(8,128)S(1)} custom-call(f32[1,24,3072]{2,1,0:T(8,128)} %v_any.1, f32[24,3072]{1,0:T(8,128)} %diag_any.1, f32[1]{0:T(128)S(6)} %copy.8.shift_ref, f32[4,4]{1,0:T(4,128)S(1)} %copy-done.1, bf16[240,128]{1,0:T(8,128)(2,1)} %mine_ref.1, s32[10,24]{1,0:T(8,128)S(1)} %bitcast.3), custom_call_target="tpu_custom_call" | custom-call | tf_op jit(solution)/shard_map/filter/pallas_call | solution.py:610
  99.4 0.7 copy.9
Async XLA Ops:
  0.0 0.7 copy-start.1
  0.7 0.7 copy-start

commit v7 on v6

--- a/solution.py
+++ b/solution.py
@@ -595,6 +595,10 @@
         sent_z(kind, ref)
 
 
+def kept(value):
+    return pltpu.with_memory_space_constraint(value, pltpu.HBM)
+
+
 def shards(coeffs, diagonal, shift, rotation, string_blocks, block_cols):
     vmem = pl.BlockSpec(memory_space=pltpu.VMEM)
     smem = pl.BlockSpec(memory_space=pltpu.SMEM)
@@ -629,8 +633,7 @@
         compiler_params=pltpu.CompilerParams(
             collective_id=0, has_side_effects=True, vmem_limit_bytes=50331648),
         name="filter",
-    )(*(pltpu.with_memory_space_constraint(a, pltpu.HBM) for a in (coeffs, diagonal)), shift, rotation,
-      pltpu.with_memory_space_constraint(string_blocks, pltpu.HBM), block_cols.T)
+    )(kept(coeffs), kept(diagonal), shift, kept(rotation), kept(string_blocks), kept(block_cols.T))
     return result[None]
 
 

time: 100 us -> 100 us (level)
  no operation moved by 1% of the time
where the time goes in v7:
time: 100 us
  Pallas kernels  98.6 us (99%)
    pallas_call x1, Pallas kernels, shards(): pl.pallas_call(kernel, out_shape=jax.ShapeDtypeStruct((24, 3072), F32), i...  98.6 us

profile of v7, /device:TPU:1, one launch (start us, length us, event | category | flops | bytes accessed | tf_op | source)
XLA Modules:
  0.0 100.0 jit_solution(1799080902450908399)
XLA Ops:
  0.7 98.6 %filter.1 = f32[24,3072]{1,0:T(8,128)S(1)} custom-call(f32[1,24,3072]{2,1,0:T(8,128)} %v_any.1, f32[24,3072]{1,0:T(8,128)} %diag_any.1, f32[1]{0:T(128)S(6)} %copy.8.shift_ref, f32[4,4]{1,0:T(4,128)} %rot_ref.1, bf16[240,128]{1,0:T(8,128)(2,1)} %mine_ref.1, s32[10,24]{1,0:T(8,128)} %bitcast.3), custom_call_target="tpu_custom_call" | custom-call | tf_op jit(solution)/shard_map/filter/pallas_call | solution.py:614
  99.3 0.7 copy.9
